TPU v7x, 512 devices: a whole 4x8x8 slice. The times are simulated.
512 devices in a mesh: gx: 64 (over x, z_lo, y), gy: 8 (over z_hi, core).
Axes of the slice: x: 4, y: 8, z: 8 (z_hi: 4, z_lo: 2; z = z_hi * 2 + z_lo), core: 2. Of those that a mesh axis runs over, the one named last changes fastest.
Arguments:
- flow_field: bfloat16 [256, 128, 64, 128], P('gx', 'gy'), may hold values from -6 to 6
- spectral_weight: bfloat16 [512, 64, 2, 64, 128], P(('gy', 'gx')), may hold values from -1 to 1
- conv_weight: bfloat16 [3, 3, 3, 128, 128], replicated, may hold values from -0.109375 to 0.109375
- channel_bias: float32 [128], replicated, may hold values from -3 to 3
Outputs:
- activated: bfloat16 [256, 128, 64, 128], P('gx', 'gy')
All inputs are finite; a program needn't handle non-finite values.
Results may differ from a plain program's by a relative error of at most 0.018.
Values may be sent and summed in bfloat16 or wider, within the bound.
A program may use at most 128 MiB of HBM per device.

v0:
```python
import math

import jax
import jax.numpy as jnp
from jax import lax
from jax.sharding import PartitionSpec as P

MX = 64
MY = 16
MZ = 16


def with_halo(array, sides, width):
    for axis, dim in sides:
        size, length = (lax.axis_size(axis), array.shape[dim])
        up = [(i, (i + 1) % size) for i in range(size - 1)]
        down = [(j, i) for i, j in up]
        last = lax.slice_in_dim(array, length - width, length, axis=dim)
        initial = lax.slice_in_dim(array, 0, width, axis=dim)
        before = lax.ppermute(last, axis, up)
        after = lax.ppermute(initial, axis, down)
        array = jnp.concatenate([before, array, after], axis=dim)
    return array


def signed_modes(mode_count):
    position = jnp.arange(mode_count, dtype=jnp.int32)
    return jnp.where(position < mode_count // 2, position, position - mode_count)


def angle_grid(first, second, length):
    phase_turns = first[:, None] * second[None, :] % length
    return phase_turns.astype(jnp.float32) * (2.0 * math.pi / length)


def real_table(first, second, length, factor):
    angles = angle_grid(first, second, length)
    return jnp.stack([jnp.cos(angles) * factor, -jnp.sin(angles) * factor])


def complex_table(first, second, length, factor, direction):
    angles = angle_grid(first, second, length)
    cosine = jnp.cos(angles) * factor
    sine_part = jnp.sin(angles) * factor
    return jnp.stack(
        [jnp.stack([cosine, direction * sine_part]), jnp.stack([-direction * sine_part, cosine])]
    )


def spectral_part(flow_field, spectral_weight):
    highest = lax.Precision.HIGHEST
    cells_x, cells_y, cells_z, channels = flow_field.shape
    count_x = lax.axis_size("gx")
    count_y = lax.axis_size("gy")
    full_x = cells_x * count_x
    full_y = cells_y * count_y
    item_count = spectral_weight.shape[0]
    local_y = lax.axis_index("gy") * cells_y + jnp.arange(cells_y, dtype=jnp.int32)
    grid_x = jnp.arange(full_x, dtype=jnp.int32)
    grid_z = jnp.arange(cells_z, dtype=jnp.int32)
    modes_z = jnp.arange(MZ, dtype=jnp.int32)
    forward_z = real_table(grid_z, modes_z, cells_z, cells_z ** (-0.5)).astype(jnp.bfloat16)
    z_spectrum = jnp.einsum(
        "xyzc,pzk->pxykc", flow_field, forward_z, preferred_element_type=jnp.float32
    )
    forward_y = complex_table(local_y, signed_modes(MY), full_y, full_y ** (-0.5), -1.0)
    y_partial = jnp.einsum("pxykc,pqyj->qxjkc", z_spectrum, forward_y, precision=highest)
    y_partial = y_partial.reshape(2, cells_x, count_y, count_x, item_count, channels // 2)
    owned = lax.psum_scatter(
        y_partial.astype(jnp.bfloat16), "gy", scatter_dimension=2, tiled=True
    ).astype(jnp.float32)
    owned_modes = owned.reshape(2, cells_x, count_x, item_count, channels // 2)
    gathered_rows = lax.all_to_all(
        owned_modes.astype(jnp.bfloat16), "gx", split_axis=2, concat_axis=1, tiled=True
    ).astype(owned_modes.dtype)
    gathered_rows = gathered_rows.reshape(2, full_x, item_count, channels // 2)
    forward_x = complex_table(grid_x, signed_modes(MX), full_x, full_x ** (-0.5), -1.0)
    x_spectrum = jnp.einsum("pxjc,pqxm->qmjc", gathered_rows, forward_x, precision=highest).astype(
        jnp.bfloat16
    )
    products = jnp.einsum(
        "pmjc,jmqco->pqmjo", x_spectrum, spectral_weight, preferred_element_type=jnp.float32
    )
    mixed_modes = jnp.stack([products[0, 0] - products[1, 1], products[0, 1] + products[1, 0]])
    backward_x = complex_table(signed_modes(MX), grid_x, full_x, MX ** (-0.5), 1.0)
    inverse_x = jnp.einsum("pmjc,pqmx->qxjc", mixed_modes, backward_x, precision=highest)
    inverse_x = inverse_x.reshape(2, full_x, 1, item_count, channels)
    returned = lax.all_to_all(
        inverse_x.astype(jnp.bfloat16), "gx", split_axis=1, concat_axis=2, tiled=True
    ).astype(inverse_x.dtype)
    band_rows = MY // count_y
    summed = returned.reshape(2, cells_x, band_rows * MZ, 2, channels).sum(axis=3)
    summed = summed.reshape(2, cells_x, band_rows, MZ, channels)
    coefficients = lax.all_gather(summed.astype(jnp.bfloat16), "gy", axis=2, tiled=True).astype(
        summed.dtype
    )
    backward_y = complex_table(signed_modes(MY), local_y, full_y, MY ** (-0.5), 1.0)
    y_inverse = jnp.einsum("pxjkc,pqjy->qxykc", coefficients, backward_y, precision=highest).astype(
        jnp.bfloat16
    )
    backward_z = real_table(modes_z, grid_z, cells_z, MZ ** (-0.5)).astype(jnp.bfloat16)
    return jnp.einsum("pxykc,pkz->xyzc", y_inverse, backward_z, preferred_element_type=jnp.float32)


def convolve(flow_field, conv_weight):
    cells_x, cells_y, cells_z, channels = flow_field.shape
    padded = with_halo(flow_field, (("gx", 0), ("gy", 1)), 1)
    padded = jnp.pad(padded, ((0, 0), (0, 0), (1, 1), (0, 0)))
    stacked = jnp.concatenate(
        [padded[:, :, 0:cells_z], padded[:, :, 1 : cells_z + 1], padded[:, :, 2 : cells_z + 2]],
        axis=3,
    )
    kernel = conv_weight.reshape(3, 3, 3 * channels, channels)
    accumulated = jnp.zeros((cells_x, cells_y, cells_z, channels), jnp.float32)
    for shift_x in range(3):
        for shift_y in range(3):
            accumulated = accumulated + jnp.dot(
                stacked[shift_x : shift_x + cells_x, shift_y : shift_y + cells_y],
                kernel[shift_x, shift_y],
                preferred_element_type=jnp.float32,
            )
    return accumulated


def body(flow_field, spectral_weight, conv_weight, channel_bias):
    convolved = convolve(flow_field, conv_weight)
    spectral = spectral_part(flow_field, spectral_weight)
    return jax.nn.gelu(spectral + convolved + channel_bias, approximate=True).astype(jnp.bfloat16)


def solution(mesh):
    placed = (P("gx", "gy", None, None), P(("gy", "gx"), None, None, None, None), P(), P())
    return jax.shard_map(
        body, mesh=mesh, in_specs=placed, out_specs=P("gx", "gy", None, None), check_vma=False
    )
```

profile of v0, /device:TPU:1, one launch (start us, length us, event | category | flops | bytes accessed | tf_op | source)
XLA Modules:
  0.0 191.2 jit_solution(16741173766615642969)
XLA Ops:
  6.5 2.0 %fusion.100 = (bf16[1,16,64,128]{3,2,1,0:T(8,128)(2,1)}, bf16[1,16,64,128]{3,2,1,0:T(8,128)(2,1)}) fusion(bf16[4,16,64,128]{3,2,1,0:T(8,128)(2,1)} %param.4), kind=kLoop, calls=%fused_computation.177 | loop fusion | bytes 1048576 | tf_op jit(solution)/shard_map/slice | solution.py:19
  9.9 5.4 %collective-permute-start = (bf16[1,16,64,128]{3,2,1,0:T(8,128)(2,1)}, bf16[1,16,64,128]{3,2,1,0:T(8,128)(2,1)}, u32[]{:S(2)}, u32[]{:S(2)}) collective-permute-start(bf16[1,16,64,128]{3,2,1,0:T(8,128)(2,1)} %get-tuple-element.10), channel_id=1, source_target_pairs={{0,8},{8,16},{16,24},{24,32},{32,40},{40,48},{48,56},{56,64},{64,7... | collective-permute-start | bytes 786440 | tf_op jit(solution)/shard_map/ppermute | solution.py:20
  16.1 1.5 convolution_bitcast_fusion.2
  19.8 2.5 %convert_element_type.204 = bf16[2,4,8,64,1,64]{5,3,2,1,0,4:T(8,128)(2,1)} reshape(bf16[2,4,16,16,128]{4,3,2,1,0:T(8,128)(2,1)} %copy.48) | data formatting | bytes 1048576 | tf_op jit(solution)/shard_map/convert_element_type | solution.py:70
  28.5 7.1 %collective-permute-start.2 = (bf16[6,1,64,128]{3,2,1,0:T(8,128)(2,1)S(1)}, bf16[6,1,64,128]{3,2,1,0:T(8,128)(2,1)S(1)}, u32[]{:S(2)}, u32[]{:S(2)}) collective-permute-start(bf16[6,1,64,128]{3,2,1,0:T(8,128)(2,1)S(1)} %get-tuple-element.7), channel_id=1, source_target_pairs={{0,1},{1,2},{2,3},{3,4},{4,5},{5,6},{6,7},{8,9},{9,10},{10,11},{11... | collective-permute-start | bytes 294920 | tf_op jit(solution)/shard_map/ppermute | solution.py:20
  35.6 2.9 %collective-permute-start.3 = (bf16[6,1,64,128]{3,2,1,0:T(8,128)(2,1)S(1)}, bf16[6,1,64,128]{3,2,1,0:T(8,128)(2,1)S(1)}, u32[]{:S(2)}, u32[]{:S(2)}) collective-permute-start(bf16[6,1,64,128]{3,2,1,0:T(8,128)(2,1)S(1)} %get-tuple-element.8), channel_id=1, source_target_pairs={{1,0},{2,1},{3,2},{4,3},{5,4},{6,5},{7,6},{9,8},{10,9},{11,10},{12... | collective-permute-start | bytes 294920 | tf_op jit(solution)/shard_map/ppermute | solution.py:21
  39.1 3.3 %collective-permute-done.3 = bf16[6,1,64,128]{3,2,1,0:T(8,128)(2,1)S(1)} collective-permute-done((bf16[6,1,64,128]{3,2,1,0:T(8,128)(2,1)S(1)}, bf16[6,1,64,128]{3,2,1,0:T(8,128)(2,1)S(1)}, u32[]{:S(2)}, u32[]{:S(2)}) %collective-permute-start.3) | collective-permute-done | bytes 98336 | tf_op jit(solution)/shard_map/ppermute | solution.py:21
  45.8 2.7 %fusion.41 = f32[4,16,64,128]{3,2,1,0:T(8,128)} fusion(bf16[6,18,64,384]{3,2,1,0:T(8,128)(2,1)S(1)} %pad_maximum_fusion, bf16[3,3,384,128]{3,2,1,0:T(8,128)(2,1)S(1)} %bitcast.222), kind=kOutput, calls=%fused_computation.56 | convolution fusion | flops 402653184 | bytes 7503872 | tf_op jit(solution)/shard_map/dot_general | solution.py:117
  48.5 2.3 %fusion.42 = f32[4,16,64,128]{3,2,1,0:T(8,128)} fusion(bf16[6,18,64,384]{3,2,1,0:T(8,128)(2,1)S(1)} %pad_maximum_fusion, bf16[3,3,384,128]{3,2,1,0:T(8,128)(2,1)S(1)} %bitcast.223), kind=kOutput, calls=%fused_computation.58 | convolution fusion | flops 402653184 | bytes 7503872 | tf_op jit(solution)/shard_map/dot_general | solution.py:117
  50.8 2.3 %fusion.43 = f32[4,16,64,128]{3,2,1,0:T(8,128)} fusion(bf16[6,18,64,384]{3,2,1,0:T(8,128)(2,1)S(1)} %pad_maximum_fusion, bf16[3,3,384,128]{3,2,1,0:T(8,128)(2,1)S(1)} %bitcast.224), kind=kOutput, calls=%fused_computation.60 | convolution fusion | flops 402653184 | bytes 7503872 | tf_op jit(solution)/shard_map/dot_general | solution.py:117
  53.1 2.4 %fusion.44 = f32[4,16,64,128]{3,2,1,0:T(8,128)} fusion(bf16[6,18,64,384]{3,2,1,0:T(8,128)(2,1)S(1)} %pad_maximum_fusion, bf16[3,3,384,128]{3,2,1,0:T(8,128)(2,1)S(1)} %bitcast.225), kind=kOutput, calls=%fused_computation.62 | convolution fusion | flops 402653184 | bytes 7503872 | tf_op jit(solution)/shard_map/dot_general | solution.py:117
  55.5 2.3 %fusion.45 = f32[4,16,64,128]{3,2,1,0:T(8,128)} fusion(bf16[6,18,64,384]{3,2,1,0:T(8,128)(2,1)S(1)} %pad_maximum_fusion, bf16[3,3,384,128]{3,2,1,0:T(8,128)(2,1)S(1)} %bitcast.226), kind=kOutput, calls=%fused_computation.64 | convolution fusion | flops 402653184 | bytes 7503872 | tf_op jit(solution)/shard_map/dot_general | solution.py:117
  57.8 2.4 %fusion.46 = f32[4,16,64,128]{3,2,1,0:T(8,128)} fusion(bf16[6,18,64,384]{3,2,1,0:T(8,128)(2,1)S(1)} %pad_maximum_fusion, bf16[3,3,384,128]{3,2,1,0:T(8,128)(2,1)S(1)} %bitcast.227), kind=kOutput, calls=%fused_computation.66 | convolution fusion | flops 402653184 | bytes 7503872 | tf_op jit(solution)/shard_map/dot_general | solution.py:117
  60.2 49.9 %all-reduce.4.cloned.1.call-done = bf16[2,4,8,64,1,64]{5,3,2,1,0,4:T(8,128)(2,1)} async-done(((bf16[2,4,8,64,1,64]{5,3,2,1,0,4:T(8,128)(2,1)}), bf16[2,4,8,64,1,64]{5,3,2,1,0,4:T(8,128)(2,1)}) %all-reduce.4.cloned.1.call-update) | async-done | bytes 524304
  112.4 1.7 reshape.950
  114.1 10.7 %all-to-all-start = ((bf16[64,2,256]{2,1,0:T(2,128)(2,1)}), bf16[64,2,256]{2,1,0:T(2,128)(2,1)}, u32[]{:S(2)}, u32[]{:S(2)}) async-start(bf16[64,2,256]{2,1,0:T(2,128)(2,1)} %reshape.950), calls=%async_computation | async-start | bytes 131072 | tf_op jit(solution)/shard_map/all_to_all | solution.py:73
  124.8 4.2 %fusion.47 = f32[4,16,64,128]{3,2,1,0:T(8,128)} fusion(bf16[6,18,64,384]{3,2,1,0:T(8,128)(2,1)} %copy-done.1, bf16[3,3,384,128]{3,2,1,0:T(8,128)(2,1)S(1)} %bitcast.228), kind=kOutput, calls=%fused_computation.68 | convolution fusion | flops 402653184 | bytes 7503872 | tf_op jit(solution)/shard_map/dot_general | solution.py:117
  129.0 4.9 %all-to-all-done = bf16[64,2,256]{2,1,0:T(2,128)(2,1)} async-done(((bf16[64,2,256]{2,1,0:T(2,128)(2,1)}), bf16[64,2,256]{2,1,0:T(2,128)(2,1)}, u32[]{:S(2)}, u32[]{:S(2)}) %all-to-all-start) | async-done | bytes 65568 | tf_op jit(solution)/shard_map/all_to_all | solution.py:73
  134.0 1.7 reshape.951
  138.8 5.7 %all-to-all-start.1 = ((bf16[2,256,1,1,128]{4,0,3,2,1:T(2,128)(2,1)}), bf16[2,256,1,1,128]{4,0,3,2,1:T(2,128)(2,1)S(1)}, u32[]{:S(2)}, u32[]{:S(2)}) async-start(bf16[2,256,1,1,128]{4,0,3,2,1:T(2,128)(2,1)} %copy.55), calls=%async_computation.1 | async-start | bytes 262144 | tf_op jit(solution)/shard_map/all_to_all | solution.py:88
  144.5 4.2 %fusion.48 = f32[4,16,64,128]{3,2,1,0:T(8,128)} fusion(bf16[6,18,64,384]{3,2,1,0:T(8,128)(2,1)} %copy-done.1, bf16[3,3,384,128]{3,2,1,0:T(8,128)(2,1)S(1)} %bitcast.229), kind=kOutput, calls=%fused_computation.70 | convolution fusion | flops 402653184 | bytes 7503872 | tf_op jit(solution)/shard_map/dot_general | solution.py:117
  148.7 5.8 %all-to-all-done.1 = bf16[2,256,1,1,128]{4,0,3,2,1:T(2,128)(2,1)S(1)} async-done(((bf16[2,256,1,1,128]{4,0,3,2,1:T(2,128)(2,1)}), bf16[2,256,1,1,128]{4,0,3,2,1:T(2,128)(2,1)S(1)}, u32[]{:S(2)}, u32[]{:S(2)}) %all-to-all-start.1) | async-done | bytes 131104 | tf_op jit(solution)/shard_map/all_to_all | solution.py:88
  154.7 19.6 %all_gather.3 = bf16[2,4,16,16,128]{4,3,1,0,2:T(8,128)(2,1)S(1)} all-gather(bf16[2,4,2,16,128]{4,3,1,0,2:T(8,128)(2,1)S(1)} %copy.58), channel_id=1, replica_groups=mesh['gx'=64,'gy'=8] {'gy'}, dimensions={2}, use_global_device_ids=true | all-gather | bytes 589824 | tf_op jit(solution)/shard_map/all_gather | solution.py:94
  175.6 8.8 %fusion.11 = bf16[4,16,64,128]{3,2,1,0:T(8,128)(2,1)} fusion(f32[64,4,16,128,1]{3,0,4,2,1:T(8,128)S(1)} %fusion.32, f32[4,16,64,128]{3,2,1,0:T(8,128)S(1)} %copy-done.2, f32[4,16,64,128]{3,2,1,0:T(8,128)S(1)} %copy-done.3, f32[4,16,64,128]{3,2,1,0:T(8,128)} %fusion.43, f32[4,16,64,128]{3,2,1,0:T(8,128)} %fusion.44, f32[4,16,64,128]{3,2,1,0:T(8,128)} %fusion.45, ...), kind=kOutput, calls=%fused_computation.15 | convolution fusion | flops 412614656 | bytes 25330176 | tf_op jit(solution)/shard_map/dot_general | solution.py:117
  (64 shorter events, 21.2 us)
Async XLA Ops:
  6.5 130.4 %copy-start = (bf16[1,64,2,64,128]{4,3,2,1,0:T(8,128)(2,1)S(1)}, bf16[1,64,2,64,128]{4,3,2,1,0:T(8,128)(2,1)}, u32[]{:S(2)}) copy-start(bf16[1,64,2,64,128]{4,3,2,1,0:T(8,128)(2,1)} %param.5) | copy-start | bytes 6291460
  6.5 103.6 %all-reduce.4.cloned.1.call-start = ((), (), s32[]{:S(2)}) async-start(), calls=%async_computation.2 | async-start | bytes 2097152
  8.6 18.9 %collective-permute-start.1 = (bf16[1,16,64,128]{3,2,1,0:T(8,128)(2,1)}, bf16[1,16,64,128]{3,2,1,0:T(8,128)(2,1)}, u32[]{:S(2)}, u32[]{:S(2)}) collective-permute-start(bf16[1,16,64,128]{3,2,1,0:T(8,128)(2,1)} %get-tuple-element.9), channel_id=1, source_target_pairs={{8,0},{16,8},{24,16},{32,24},{40,32},{48,40},{56,48},{64,56},{72,6... | collective-permute-start | bytes 786440 | tf_op jit(solution)/shard_map/ppermute | solution.py:21
  9.9 16.5 %collective-permute-start = (bf16[1,16,64,128]{3,2,1,0:T(8,128)(2,1)}, bf16[1,16,64,128]{3,2,1,0:T(8,128)(2,1)}, u32[]{:S(2)}, u32[]{:S(2)}) collective-permute-start(bf16[1,16,64,128]{3,2,1,0:T(8,128)(2,1)} %get-tuple-element.10), channel_id=1, source_target_pairs={{0,8},{8,16},{16,24},{24,32},{32,40},{40,48},{48,56},{56,64},{64,7... | collective-permute-start | bytes 786440 | tf_op jit(solution)/shard_map/ppermute | solution.py:20
  19.8 7.5 %copy-start.4 = (bf16[4,16,64,128]{3,2,1,0:T(8,128)(2,1)S(1)}, bf16[4,16,64,128]{3,2,1,0:T(8,128)(2,1)}, u32[]{:S(2)}) copy-start(bf16[4,16,64,128]{3,2,1,0:T(8,128)(2,1)} %param.4) | copy-start | bytes 3145732
  28.5 10.6 %collective-permute-start.2 = (bf16[6,1,64,128]{3,2,1,0:T(8,128)(2,1)S(1)}, bf16[6,1,64,128]{3,2,1,0:T(8,128)(2,1)S(1)}, u32[]{:S(2)}, u32[]{:S(2)}) collective-permute-start(bf16[6,1,64,128]{3,2,1,0:T(8,128)(2,1)S(1)} %get-tuple-element.7), channel_id=1, source_target_pairs={{0,1},{1,2},{2,3},{3,4},{4,5},{5,6},{6,7},{8,9},{9,10},{10,11},{11... | collective-permute-start | bytes 294920 | tf_op jit(solution)/shard_map/ppermute | solution.py:20
  35.6 6.8 %collective-permute-start.3 = (bf16[6,1,64,128]{3,2,1,0:T(8,128)(2,1)S(1)}, bf16[6,1,64,128]{3,2,1,0:T(8,128)(2,1)S(1)}, u32[]{:S(2)}, u32[]{:S(2)}) collective-permute-start(bf16[6,1,64,128]{3,2,1,0:T(8,128)(2,1)S(1)} %get-tuple-element.8), channel_id=1, source_target_pairs={{1,0},{2,1},{3,2},{4,3},{5,4},{6,5},{7,6},{9,8},{10,9},{11,10},{12... | collective-permute-start | bytes 294920 | tf_op jit(solution)/shard_map/ppermute | solution.py:21
  44.6 1.2 copy-start.5
  45.5 12.4 %copy-start.1 = (bf16[6,18,64,384]{3,2,1,0:T(8,128)(2,1)}, bf16[6,18,64,384]{3,2,1,0:T(8,128)(2,1)S(1)}, u32[]{:S(2)}) copy-start(bf16[6,18,64,384]{3,2,1,0:T(8,128)(2,1)S(1)} %pad_maximum_fusion) | copy-start | bytes 15925252
  114.1 19.9 %all-to-all-start = ((bf16[64,2,256]{2,1,0:T(2,128)(2,1)}), bf16[64,2,256]{2,1,0:T(2,128)(2,1)}, u32[]{:S(2)}, u32[]{:S(2)}) async-start(bf16[64,2,256]{2,1,0:T(2,128)(2,1)} %reshape.950), calls=%async_computation | async-start | bytes 131072 | tf_op jit(solution)/shard_map/all_to_all | solution.py:73
  124.8 11.9 %copy-start.6 = (f32[1,2,256,64]{2,3,1,0:T(8,128)S(1)}, f32[1,2,256,64]{2,3,1,0:T(8,128)}, u32[]{:S(2)}) copy-start(f32[1,2,256,64]{2,3,1,0:T(8,128)} %get-tuple-element.15) | copy-start | bytes 393220
  138.8 15.7 %all-to-all-start.1 = ((bf16[2,256,1,1,128]{4,0,3,2,1:T(2,128)(2,1)}), bf16[2,256,1,1,128]{4,0,3,2,1:T(2,128)(2,1)S(1)}, u32[]{:S(2)}, u32[]{:S(2)}) async-start(bf16[2,256,1,1,128]{4,0,3,2,1:T(2,128)(2,1)} %copy.55), calls=%async_computation.1 | async-start | bytes 262144 | tf_op jit(solution)/shard_map/all_to_all | solution.py:88
  144.5 29.9 %copy-start.7 = (f32[1,2,16,16]{2,3,1,0:T(8,128)S(1)}, f32[1,2,16,16]{2,3,1,0:T(8,128)}, u32[]{:S(2)}) copy-start(f32[1,2,16,16]{2,3,1,0:T(8,128)} %get-tuple-element.19) | copy-start | bytes 6148
  148.7 26.4 %copy-start.8 = (bf16[1,16,64]{2,1,0:T(8,128)(2,1)S(1)}, bf16[1,16,64]{2,1,0:T(8,128)(2,1)}, u32[]{:S(2)}) copy-start(bf16[1,16,64]{2,1,0:T(8,128)(2,1)} %get-tuple-element.38) | copy-start | bytes 6148
  148.7 26.4 %copy-start.9 = (bf16[1,16,64]{2,1,0:T(8,128)(2,1)S(1)}, bf16[1,16,64]{2,1,0:T(8,128)(2,1)}, u32[]{:S(2)}) copy-start(bf16[1,16,64]{2,1,0:T(8,128)(2,1)} %get-tuple-element.39) | copy-start | bytes 6148
  154.7 20.8 %copy-start.2 = (f32[4,16,64,128]{3,2,1,0:T(8,128)S(1)}, f32[4,16,64,128]{3,2,1,0:T(8,128)}, u32[]{:S(2)}) copy-start(f32[4,16,64,128]{3,2,1,0:T(8,128)} %fusion.41) | copy-start | bytes 6291460
  154.7 20.8 %copy-start.3 = (f32[4,16,64,128]{3,2,1,0:T(8,128)S(1)}, f32[4,16,64,128]{3,2,1,0:T(8,128)}, u32[]{:S(2)}) copy-start(f32[4,16,64,128]{3,2,1,0:T(8,128)} %fusion.42) | copy-start | bytes 6291460
  154.7 20.8 %copy-start.10 = (f32[128]{0:T(128)S(1)}, f32[128]{0:T(128)}, u32[]{:S(2)}) copy-start(f32[128]{0:T(128)} %param.7) | copy-start | bytes 1540
Sparse Core Ops, SparseCore 0:
  22.4 87.7 all-reduce.3
where the time goes:
time: 192 us; the launch traced here: 191 us
  waiting for transfers between devices  64 us (33%)
  matrix products  36.8 us (19%)
  starting transfers between devices  33 us (17%)
  blocking collectives  19.6 us (10%)
  local copies, waits for them, and re-layouts  17.5 us (9%)
  between operations  13.8 us (7%)
  other arithmetic  6.65 us (3%)
    unnamed x2, waiting for transfers between devices  49.9 us
    dot_general x9, matrix products, convolve(): jnp.dot(stacked[shift_x:shift_x + cells_x, shift_y:shift_y + cells_y], ke...  31.7 us
    all_gather x1, blocking collectives, spectral_part(): lax.all_gather(summed.astype(jnp.bfloat16), 'gy', axis=2, tiled=True)  19.6 us
    ppermute x2, starting transfers between devices, with_halo(): before = lax.ppermute(last, axis, up)  12.5 us
    all_to_all x1, starting transfers between devices, spectral_part(): lax.all_to_all(owned_modes.astype(jnp.bfloat16), 'gx', split_axis=2, conc...  10.7 us
    unnamed x28, local copies, waits for them, and re-layouts  6.05 us
    all_to_all x1, waiting for transfers between devices, spectral_part(): lax.all_to_all(inverse_x.astype(jnp.bfloat16), 'gx', split_axis=1, concat...  5.77 us
    all_to_all x1, starting transfers between devices, spectral_part(): lax.all_to_all(inverse_x.astype(jnp.bfloat16), 'gx', split_axis=1, concat...  5.67 us
  transfers between devices with their start and end apart: 7, of which 4 were waited for; matrix products, arithmetic and copies ran while one was open for 21% of the time, Pallas kernels for 0%

commit v1 on v0

v1 whole, which is shorter than its diff:
```python
import functools
import math

import jax
import jax.numpy as jnp
import numpy as np
from jax import lax
from jax.experimental import pallas as pl
from jax.experimental.pallas import tpu as pltpu
from jax.sharding import PartitionSpec as P

MX = 64
MY = 16
MZ = 16
MESH = pl.DeviceIdType.MESH
ANY = pl.BlockSpec(memory_space=pl.ANY)
BF = jnp.bfloat16
F32 = jnp.float32


def signed(count):
    position = np.arange(count)
    return np.where(position < count // 2, position, position - count)


def angles(first, second, length):
    return (np.multiply.outer(first, second) % length) * (2.0 * math.pi / length)


def rounded(values):
    return np.asarray(values, dtype=BF)


def tables(count_x, count_y, cells_x, cells_y, cells_z):
    full_x, full_y = count_x * cells_x, count_y * cells_y
    half = count_y // 2
    theta = angles(np.arange(cells_z), np.arange(MZ), cells_z)
    forward = [
        rounded(f(theta) * s * cells_z**-0.5).astype(np.float64) for f, s in ((np.cos, 1), (np.sin, -1))
    ]
    backward = [
        rounded(f(theta) * s * MZ**-0.5).astype(np.float64) for f, s in ((np.cos, 1), (np.sin, -1))
    ]
    phi = angles(signed(MY), np.arange(cells_y), full_y)
    cos, sin = np.cos(phi), np.sin(phi)
    outer = lambda a, b: np.einsum("jy,zk->jkyz", a, b)
    a_re = (outer(cos, forward[0]) + outer(sin, forward[1])) * full_y**-0.5
    a_im = (outer(cos, forward[1]) - outer(sin, forward[0])) * full_y**-0.5
    b_re = (outer(cos, backward[0]) + outer(sin, backward[1])) * MY**-0.5
    b_im = (outer(cos, backward[1]) - outer(sin, backward[0])) * MY**-0.5
    band = MY // count_y
    cells = cells_y * cells_z
    split = (half, 2, band, MZ, cells)
    a = np.stack([a_re.reshape(split), a_im.reshape(split)])
    a = a.transpose(2, 1, 0, 3, 4, 5).reshape(2 * MY * MZ, cells)
    b = np.stack([b_re.reshape(split), b_im.reshape(split)])
    b = b.transpose(0, 2, 1, 3, 4, 5).reshape(2 * MY * MZ, cells).T
    theta = angles(signed(MX), np.arange(full_x), full_x)
    t = np.concatenate([np.cos(theta), np.sin(theta)]) * full_x**-0.5
    cos, sin = np.cos(theta.T), np.sin(theta.T)
    ix = np.stack([np.stack([cos, -sin]), np.stack([sin, cos])]) * MX**-0.5
    ix = ix.reshape(2, 2, count_x, cells_x, MX // 8, 8).transpose(2, 0, 3, 4, 1, 5)
    ix = ix.reshape(2 * full_x, 2 * MX)
    return tuple(rounded(v) for v in (a, b, t, ix))


def eighth(t):
    r = math.sqrt(0.5)

    def value(t):
        return jnp.where(
            t == 0,
            1.0,
            jnp.where(
                t == 4,
                -1.0,
                jnp.where((t == 2) | (t == 6), 0.0, jnp.where((t == 1) | (t == 7), r, -r)),
            ),
        ).astype(F32)

    return value(t), value((t + 6) % 8)


def kernel(
    nx, ny,
    flow, weight, conv_w, bias, a_hbm, b_hbm, t_hbm, ix_hbm,
    out,
    pad, w_v, cw_v, a_v, b_v, t_v, ix_v, brot,
    snd1, own1, rcv1, snd2, rcv2, stage, snda, rcva, sndb, rcvb, coef, conv,
    load_sem, halo_s, halo_r, pair_s, pair_r, ring_s, ring_r, a2a_s, a2a_r, ag_s, ag_r, fw_s, fw_r,
):
    gx, gy = lax.axis_index("gx"), lax.axis_index("gy")
    zh, core = gy // 2, gy % 2
    nz = ny // 2
    cx = flow.shape[0]
    cy = flow.shape[1]
    cz = flow.shape[2]
    cells = cy * cz

    loads = [
        pltpu.make_async_copy(flow, pad.at[pl.ds(1, cx), pl.ds(1, cy)], load_sem.at[0]),
        pltpu.make_async_copy(a_hbm, a_v, load_sem.at[1]),
        pltpu.make_async_copy(conv_w, cw_v, load_sem.at[2]),
        pltpu.make_async_copy(b_hbm, b_v, load_sem.at[3]),
        pltpu.make_async_copy(t_hbm, t_v, load_sem.at[4]),
        pltpu.make_async_copy(ix_hbm, ix_v, load_sem.at[5]),
        pltpu.make_async_copy(weight, w_v, load_sem.at[6]),
    ]
    for load in loads:
        load.start()

    barrier = pltpu.get_barrier_semaphore()

    def greet(i, carry):
        pl.semaphore_signal(
            barrier, inc=1, device_id=((gx + i) % nx, gy), device_id_type=MESH
        )
        return carry

    lax.fori_loop(1, nx, greet, 0)
    partner = gy + 1 - 2 * core
    beside = (gy + ny - 1 + 2 * core) % ny
    for d in range(1, nz):
        pl.semaphore_signal(
            barrier, inc=1, device_id=(gx, ((zh + d) % nz) * 2 + core), device_id_type=MESH
        )
    for y in (partner, beside):
        for dx in (0, 1, nx - 1):
            pl.semaphore_signal(
                barrier, inc=1, device_id=((gx + dx) % nx, y), device_id_type=MESH
            )

    zero_plane = jnp.zeros((cy + 2, cz, 128), BF)
    zero_row = jnp.zeros((cx + 2, 1, cz, 128), BF)

    @pl.when(gx == 0)
    def _():
        pad[0] = zero_plane

    @pl.when(gx == nx - 1)
    def _():
        pad[cx + 1] = zero_plane

    @pl.when(gy == 0)
    def _():
        pad[:, 0:1] = zero_row

    @pl.when(gy == ny - 1)
    def _():
        pad[:, cy + 1 : cy + 2] = zero_row

    loads[0].wait()
    loads[1].wait()

    def forward(half, save):
        base = pl.multiple_of(half * (ny // 2) * 64, (ny // 2) * 64)
        rows = a_v[pl.ds(base, nz * 64), :]
        spins = [[eighth(((2 * (2 * z + half) + j2) * gy) % 8) for j2 in range(2)] for z in range(nz)]
        for xp in range(cx // 2):
            rhs = jnp.concatenate(
                [pad[1 + 2 * xp + i, 1 : cy + 1].reshape(cells, 128) for i in range(2)], axis=1
            )
            y = jnp.dot(rows, rhs, preferred_element_type=F32)
            for z in range(nz):
                for j2 in range(2):
                    c, s = spins[z][j2]
                    r0 = z * 64 + j2 * 16
                    re, im = y[r0 : r0 + 16], y[r0 + 32 : r0 + 48]
                    save(r0, xp, c * re + s * im)
                    save(r0 + 32, xp, c * im - s * re)

    def save_send(r0, xp, v):
        snd1[r0 : r0 + 16, xp * 256 : xp * 256 + 256] = v.astype(BF)

    def save_own(r0, xp, v):
        own1[r0 : r0 + 16, xp * 256 : xp * 256 + 256] = v

    forward(1 - core, save_send)

    pl.semaphore_wait(barrier, nx - 1 + nz - 1 + 6)

    pair = pltpu.make_async_remote_copy(
        src_ref=snd1, dst_ref=rcv1, send_sem=pair_s, recv_sem=pair_r,
        device_id=(gx, partner), device_id_type=MESH,
    )
    pair.start()

    inner_x, inner_y = pl.ds(1, cx), pl.ds(1, cy)

    def place(step, count, inner, send):
        if step == 0:
            return inner
        edge = (count if step > 0 else 1) if send else (0 if step > 0 else count + 1)
        return pl.ds(edge, 1)

    halos = []
    for n, (dx, dy) in enumerate(
        ((0, 1), (0, -1), (1, 1), (1, -1), (-1, 1), (-1, -1), (1, 0), (-1, 0))
    ):
        ok_send = (gx + dx >= 0) & (gx + dx < nx) & (gy + dy >= 0) & (gy + dy < ny)
        ok_recv = (gx - dx >= 0) & (gx - dx < nx) & (gy - dy >= 0) & (gy - dy < ny)
        copy = pltpu.make_async_remote_copy(
            src_ref=pad.at[place(dx, cx, inner_x, True), place(dy, cy, inner_y, True)],
            dst_ref=pad.at[place(dx, cx, inner_x, False), place(dy, cy, inner_y, False)],
            send_sem=halo_s.at[n], recv_sem=halo_r.at[n],
            device_id=((gx + dx + nx) % nx, (gy + dy + ny) % ny), device_id_type=MESH,
        )
        halos.append((copy, ok_send, ok_recv))

        @pl.when(ok_send)
        def _(copy=copy):
            copy.start()

    forward(core, save_own)

    pair.wait()
    ring = []
    for d in (2, 1, 3):
        target = (zh + d) % nz
        rows = pl.ds(pl.multiple_of(target * 64, 64), 64)
        snd2[rows, :] = (own1[rows, :] + rcv1[rows, :].astype(F32)).astype(BF)
        copy = pltpu.make_async_remote_copy(
            src_ref=snd2.at[rows], dst_ref=rcv2.at[d - 1],
            send_sem=ring_s.at[d - 1], recv_sem=ring_r.at[d - 1],
            device_id=(gx, target * 2 + core), device_id_type=MESH,
        )
        copy.start()
        ring.append(copy)

    loads[2].wait()

    def conv_block(x, m):
        steps = 4
        rows_y = cy // steps
        lhs = jnp.concatenate(
            [
                pad[x + a, pl.ds(m * rows_y + b, rows_y)].reshape(rows_y * cz, 128)
                for a in range(3)
                for b in range(3)
            ],
            axis=1,
        )
        rhs = jnp.concatenate(
            [jnp.concatenate([cw_v[ab * 3 + d] for d in range(3)], axis=1) for ab in range(9)], axis=0
        )
        acc = jnp.dot(lhs, rhs, preferred_element_type=F32)
        z = lax.broadcasted_iota(jnp.int32, (rows_y * cz, 128), 0) % cz
        low = pltpu.roll(acc[:, 0:128], 1, axis=0)
        high = pltpu.roll(acc[:, 256:384], rows_y * cz - 1, axis=0)
        total = acc[:, 128:256] + jnp.where(z == 0, 0.0, low) + jnp.where(z == cz - 1, 0.0, high)
        start = pl.multiple_of(m * rows_y * cz, rows_y * cz)
        conv[x, pl.ds(start, rows_y * cz), :] = total + bias[...]

    def conv_planes(first, count):
        def step(i, carry):
            conv_block(first + i // 4, i % 4)
            return carry

        lax.fori_loop(0, count * 4, step, 0)

    def wait_halos(which):
        for n in which:
            copy, ok_send, ok_recv = halos[n]

            @pl.when(ok_recv)
            def _(copy=copy):
                copy.wait_recv()

            @pl.when(ok_send)
            def _(copy=copy):
                copy.wait_send()

    wait_halos((0, 1))
    conv_planes(1, 2)

    for copy in ring:
        copy.wait_recv()
    rows = pl.ds(pl.multiple_of(zh * 64, 64), 64)
    lane = lax.broadcasted_iota(jnp.int32, (32, 128), 1)
    for x in range(cx):
        cols = slice(x * 128, x * 128 + 128)
        band = own1[rows, cols] + rcv1[rows, cols].astype(F32)
        for d in range(nz - 1):
            band = band + rcv2[d, :, cols].astype(F32)
        re, im = band[:32], band[32:]
        stage[pl.ds(x, 32, stride=8), :] = jnp.where(lane < 64, re, pltpu.roll(im, 64, axis=1))
        stage[pl.ds(4 + x, 32, stride=8), :] = jnp.where(lane < 64, pltpu.roll(re, 64, axis=1), im)
    snda[...] = stage[...].astype(BF).reshape(nx, 4, 128)

    def exchange(src, dst, number):
        def send(i, carry):
            to = (gx + i) % nx
            pltpu.make_async_remote_copy(
                src_ref=src.at[to], dst_ref=dst.at[gx],
                send_sem=a2a_s.at[number], recv_sem=a2a_r.at[number],
                device_id=(to, gy), device_id_type=MESH,
            ).start()
            return carry

        lax.fori_loop(1, nx, send, 0)
        dst[gx] = src[gx]

    def wait_exchange(src, dst, number):
        most = pl.ds(0, nx - 1)
        done = pltpu.make_async_remote_copy(
            src_ref=src.at[most], dst_ref=dst.at[most],
            send_sem=a2a_s.at[number], recv_sem=a2a_r.at[number],
            device_id=(gx, gy), device_id_type=MESH,
        )
        done.wait_recv()
        return done

    exchange(snda, rcva, 0)

    wait_halos((2, 3, 4, 5, 6, 7))
    conv_planes(0, 1)
    conv_planes(3, 1)
    loads[3].wait()
    lanes = lax.broadcasted_iota(jnp.int32, (1, MY * MZ), 1)
    mode = 2 * (2 * ((lanes // 32) % nz) + lanes // (32 * nz)) + (lanes // 16) % 2
    spin_c, spin_s = eighth((mode * gy) % 8)

    def rotate(i, carry):
        rows = pl.ds(pl.multiple_of(i * 64, 64), 64)
        re = b_v[rows, 0:256].astype(F32)
        im = b_v[rows, 256:512].astype(F32)
        brot[rows, 0:256] = (spin_c * re + spin_s * im).astype(BF)
        brot[rows, 256:512] = (spin_c * im - spin_s * re).astype(BF)
        return carry

    lax.fori_loop(0, cells // 64, rotate, 0)
    for load in loads[4:]:
        load.wait()

    first = wait_exchange(snda, rcva, 0)
    g = rcva[...].reshape(nx * 4, 128)
    p = jnp.dot(t_v[...], g, preferred_element_type=F32)
    lane = lax.broadcasted_iota(jnp.int32, (MX, 128), 1)
    sign = jnp.where(lane < 64, 1.0, -1.0).astype(F32)
    spec = p[:MX] + sign * pltpu.roll(p[MX:], 64, axis=1)
    row0 = spec * sign
    row1 = pltpu.roll(spec, 64, axis=1)
    sub = lax.broadcasted_iota(jnp.int32, (16, 128), 0) % 8
    mixed = []
    for blk in range(MX // 8):
        rows16 = jnp.concatenate([row0[blk * 8 : blk * 8 + 8], row1[blk * 8 : blk * 8 + 8]], axis=0)
        lhs = jnp.concatenate(
            [jnp.where(sub == i, rows16, 0.0).astype(BF) for i in range(8)], axis=1
        )
        rhs = w_v[blk * 8 : blk * 8 + 8].reshape(8 * 128, 128)
        mixed.append(jnp.dot(lhs, rhs, preferred_element_type=F32))
    mixed = jnp.concatenate(mixed, axis=0).astype(BF)
    back = jnp.dot(ix_v[...], mixed, preferred_element_type=F32)
    sndb[...] = back.astype(BF).reshape(nx, 8, 128)
    exchange(sndb, rcvb, 1)
    second = wait_exchange(sndb, rcvb, 1)

    both = rcvb[...].astype(F32).reshape(nx // 2, 2, 8, 128)
    stage[...] = (both[:, 0] + both[:, 1]).reshape(nx // 2 * 8, 128)
    slot = core * nz + zh
    for q in range(2):
        for x in range(cx):
            coef[q, slot, :, x * 128 : x * 128 + 128] = stage[
                pl.ds(q * 4 + x, 32, stride=8), :
            ].astype(BF)
    gathers = []
    for d in (2, 1, 3):
        copy = pltpu.make_async_remote_copy(
            src_ref=coef.at[:, slot], dst_ref=coef.at[:, slot],
            send_sem=ag_s.at[d - 1], recv_sem=ag_r.at[d - 1],
            device_id=(gx, ((zh + d) % nz) * 2 + core), device_id_type=MESH,
        )
        copy.start()
        gathers.append(copy)
    passes = []

    def pass_on(d):
        there = core * nz + (zh - d + nz) % nz
        copy = pltpu.make_async_remote_copy(
            src_ref=coef.at[:, there], dst_ref=coef.at[:, there],
            send_sem=fw_s.at[d], recv_sem=fw_r.at[d],
            device_id=(gx, partner), device_id_type=MESH,
        )
        copy.start()
        passes.append(copy)

    pass_on(0)
    for d, copy in ((1, gathers[1]), (3, gathers[2]), (2, gathers[0])):
        copy.wait_recv()
        pass_on(d)
    for copy in passes:
        copy.wait_recv()

    root = math.sqrt(2.0 / math.pi)
    parts = 4

    def finish(i, carry):
        size = cells // parts
        rows = pl.ds(pl.multiple_of(i * size, size), size)
        lhs = brot[rows, :]
        for xp in range(cx // 2):
            rhs = coef[:, :, :, xp * 256 : xp * 256 + 256].reshape(2 * MY * MZ, 256)
            acc = jnp.dot(lhs, rhs, preferred_element_type=F32)
            for x in range(2):
                v = acc[:, x * 128 : x * 128 + 128] + conv[2 * xp + x, rows, :]
                v = 0.5 * v * (1.0 + jnp.tanh(root * (v + 0.044715 * (v * v * v))))
                out[2 * xp + x, rows, :] = v.astype(BF)
        return carry

    lax.fori_loop(0, parts, finish, 0)

    for copy in ring + gathers + passes:
        copy.wait_send()
    first.wait_send()
    second.wait_send()


def body(consts, nx, ny, flow_field, spectral_weight, conv_weight, channel_bias):
    cells_x, cells_y, cells_z, channels = flow_field.shape
    cells = cells_y * cells_z
    nz = ny // 2
    modes = 2 * MY * MZ
    v = pltpu.VMEM
    dma = pltpu.SemaphoreType.DMA
    vmem = pl.BlockSpec(memory_space=pltpu.VMEM)
    out = pl.pallas_call(
        functools.partial(kernel, nx, ny),
        out_shape=jax.ShapeDtypeStruct((cells_x, cells, channels), BF),
        in_specs=[ANY, ANY, ANY, vmem, ANY, ANY, ANY, ANY],
        out_specs=vmem,
        scratch_shapes=[
            v((cells_x + 2, cells_y + 2, cells_z, channels), BF),
            v((MX, 128, 128), BF),
            v((27, 128, 128), BF),
            v((modes, cells), BF),
            v((cells, modes), BF),
            v((2 * MX, nx * cells_x), BF),
            v((2 * nx * cells_x, 2 * MX), BF),
            v((cells, modes), BF),
            v((modes // 2, cells_x * 128), BF),
            v((modes // 2, cells_x * 128), F32),
            v((modes // 2, cells_x * 128), BF),
            v((modes // 2, cells_x * 128), BF),
            v((nz - 1, 64, cells_x * 128), BF),
            v((256, 128), F32),
            v((nx, 4, 128), BF),
            v((nx, 4, 128), BF),
            v((nx, 8, 128), BF),
            v((nx, 8, 128), BF),
            v((2, ny, 32, cells_x * 128), BF),
            v((cells_x, cells, 128), F32),
            dma((7,)),
            dma((8,)),
            dma((8,)),
            dma,
            dma,
            dma((nz - 1,)),
            dma((nz - 1,)),
            dma((2,)),
            dma((2,)),
            dma((nz - 1,)),
            dma((nz - 1,)),
            dma((nz,)),
            dma((nz,)),
        ],
        compiler_params=pltpu.CompilerParams(collective_id=0, has_side_effects=True),
        name="layer",
    )(
        flow_field,
        spectral_weight.reshape(MX, 128, 128),
        conv_weight.reshape(27, 128, 128),
        channel_bias.reshape(1, channels),
        *consts,
    )
    return out.reshape(cells_x, cells_y, cells_z, channels)


def solution(mesh):
    nx, ny = mesh.shape["gx"], mesh.shape["gy"]
    consts = tables(nx, ny, 4, 16, 64)

    def layer(*args):
        return body(tuple(jnp.asarray(c) for c in consts), nx, ny, *args)

    placed = (P("gx", "gy", None, None), P(("gy", "gx"), None, None, None, None), P(), P())
    return jax.shard_map(
        layer, mesh=mesh, in_specs=placed, out_specs=P("gx", "gy", None, None), check_vma=False
    )
```

time: 192 us -> 62.4 us (0.33)
  waiting for transfers between devices: 64 us -> 0 us
  Pallas kernels: 0 us -> 60 us
  matrix products: 36.8 us -> 0 us
  starting transfers between devices: 33 us -> 0 us
  blocking collectives: 19.6 us -> 0 us
  local copies, waits for them, and re-layouts: 17.5 us -> 2.26 us
  between operations: 13.8 us -> 0.01 us
  other arithmetic: 6.65 us -> 0 us
    pallas_call x0 -> x1, Pallas kernels: none -> 60 us  [body(): pl.pallas_call(functools.partial(kernel, nx, ny), out_shape=jax.ShapeDtyp...]
    unnamed x2 -> x0, waiting for transfers between devices: 49.9 us -> none
    dot_general x16 -> x0, matrix products: 36.8 us -> none  [the longest x9 31.7 us: convolve(): jnp.dot(stacked[shift_x:shift_x + cells_x, shift_y:shift_y + cells_y], ke...]
    all_gather x1 -> x0, blocking collectives: 19.6 us -> none  [spectral_part(): lax.all_gather(summed.astype(jnp.bfloat16), 'gy', axis=2, tiled=True)]
    ppermute x4 -> x0, starting transfers between devices: 16.6 us -> none  [the longest x2 12.5 us: with_halo(): before = lax.ppermute(last, axis, up)]
    all_to_all x2 -> x0, starting transfers between devices: 16.4 us -> none  [the longest x1 10.7 us: spectral_part(): lax.all_to_all(owned_modes.astype(jnp.bfloat16), 'gx', split_axis=2, conc...]
    all_to_all x2 -> x0, waiting for transfers between devices: 10.7 us -> none  [the longest x1 5.77 us: spectral_part(): lax.all_to_all(inverse_x.astype(jnp.bfloat16), 'gx', split_axis=1, concat...]
    convert_element_type x6 -> x0, local copies, waits for them, and re-layouts: 6.45 us -> none  [the longest x2 3.41 us: spectral_part(): y_partial.astype(jnp.bfloat16)]
  transfers between devices with their start and end apart: 7 -> 0, of which waited for: 4 -> 0; matrix products, arithmetic and copies ran while one was open for 21% -> 0% of each run, Pallas kernels for 0% -> 0%
where the time goes in v1:
time: 62.4 us; the launch traced here: 62.3 us
  Pallas kernels  60 us (96%)
  local copies, waits for them, and re-layouts  2.26 us (4%)
    pallas_call x1, Pallas kernels, body(): pl.pallas_call(functools.partial(kernel, nx, ny), out_shape=jax.ShapeDtyp...  60 us
    unnamed x1, local copies, waits for them, and re-layouts  2.26 us

profile of v1, /device:TPU:1, one launch (start us, length us, event | category | flops | bytes accessed | tf_op | source)
XLA Modules:
  0.0 62.3 jit_solution(16640805020951356052)
XLA Ops:
  0.0 60.0 %layer.1 = bf16[4,1024,128]{2,1,0:T(8,128)(2,1)} custom-call(bf16[4,16,64,128]{3,2,1,0:T(8,128)(2,1)} %flow.1, bf16[64,128,128]{2,1,0:T(8,128)(2,1)} %bitcast.5, bf16[27,128,128]{2,1,0:T(8,128)(2,1)} %bitcast.6, f32[1,128]{1,0:T(1,128)} %bitcast.7, bf16[512,1024]{1,0:T(8,128)(2,1)} %constant.8.clone.a_hbm, bf16[1024,512]{1,0:T(8,128)(2,1)} %constant.9.clone.b_hbm, ...), custom_call_target="tpu_custom_call" | custom-call | tf_op jit(solution)/shard_map/layer/pallas_call | solution.py:426
  60.0 2.3 %copy.10 = bf16[4,16,64,128]{3,2,1,0:T(8,128)(2,1)} copy(bf16[4,16,64,128]{3,2,1,0:T(8,128)(2,1)} %bitcast.4) | data formatting | bytes 2097152

commit v2 on v1

--- a/solution.py
+++ b/solution.py
@@ -83,11 +83,11 @@
 
 def kernel(
     nx, ny,
-    flow, weight, conv_w, bias, a_hbm, b_hbm, t_hbm, ix_hbm,
+    flow, weight, conv_w, bias_hbm, a_hbm, b_hbm, t_hbm, ix_hbm,
     out,
-    pad, w_v, cw_v, a_v, b_v, t_v, ix_v, brot,
+    pad, w_v, cw_v, bias, a_v, b_v, t_v, ix_v, brot,
     snd1, own1, rcv1, snd2, rcv2, stage, snda, rcva, sndb, rcvb, coef, conv,
-    load_sem, halo_s, halo_r, pair_s, pair_r, ring_s, ring_r, a2a_s, a2a_r, ag_s, ag_r, fw_s, fw_r,
+    load_sem, wave, halo_s, halo_r, pair_s, pair_r, ring_s, ring_r, a2a_s, a2a_r, ag_s, ag_r, fw_s, fw_r,
 ):
     gx, gy = lax.axis_index("gx"), lax.axis_index("gy")
     zh, core = gy // 2, gy % 2
@@ -96,39 +96,41 @@
     cy = flow.shape[1]
     cz = flow.shape[2]
     cells = cy * cz
+    lx, lz, ly = nx // 16, 2, 8
+    at_x, at_z, at_y = gx // 16, (gx // 8) % 2, gx % 8
+    to_x = [((at_x + i) % lx) * 16 for i in range(lx)]
+    to_z = [((at_z + i) % lz) * 8 for i in range(lz)]
+    to_y = [(at_y + i) % ly for i in range(ly)]
 
     loads = [
         pltpu.make_async_copy(flow, pad.at[pl.ds(1, cx), pl.ds(1, cy)], load_sem.at[0]),
         pltpu.make_async_copy(a_hbm, a_v, load_sem.at[1]),
-        pltpu.make_async_copy(conv_w, cw_v, load_sem.at[2]),
-        pltpu.make_async_copy(b_hbm, b_v, load_sem.at[3]),
-        pltpu.make_async_copy(t_hbm, t_v, load_sem.at[4]),
-        pltpu.make_async_copy(ix_hbm, ix_v, load_sem.at[5]),
+        pltpu.make_async_copy(b_hbm, b_v, load_sem.at[2]),
+        pltpu.make_async_copy(conv_w, cw_v, load_sem.at[3]),
+        pltpu.make_async_copy(bias_hbm, bias, load_sem.at[4]),
+        pltpu.make_async_copy(t_hbm, t_v, load_sem.at[5]),
         pltpu.make_async_copy(weight, w_v, load_sem.at[6]),
+        pltpu.make_async_copy(ix_hbm, ix_v, load_sem.at[7]),
     ]
-    for load in loads:
-        load.start()
+    loads[0].start()
+    loads[1].start()
 
     barrier = pltpu.get_barrier_semaphore()
-
-    def greet(i, carry):
-        pl.semaphore_signal(
-            barrier, inc=1, device_id=((gx + i) % nx, gy), device_id_type=MESH
-        )
-        return carry
-
-    lax.fori_loop(1, nx, greet, 0)
     partner = gy + 1 - 2 * core
     beside = (gy + ny - 1 + 2 * core) % ny
-    for d in range(1, nz):
-        pl.semaphore_signal(
-            barrier, inc=1, device_id=(gx, ((zh + d) % nz) * 2 + core), device_id_type=MESH
-        )
-    for y in (partner, beside):
-        for dx in (0, 1, nx - 1):
-            pl.semaphore_signal(
-                barrier, inc=1, device_id=((gx + dx) % nx, y), device_id_type=MESH
-            )
+    next_x, last_x = (gx + 1) % nx, (gx + nx - 1) % nx
+
+    def peer(x, y):
+        return {"device_id": (x, y), "device_id_type": MESH}
+
+    greeted = [(gx, ((zh + d) % nz) * 2 + core) for d in range(1, nz)]
+    greeted += [(to_x[0] + to_z[0] + to_y[i], gy) for i in range(1, ly)]
+    greeted += [(to_x[i] + to_z[0] + to_y[0], gy) for i in range(1, lx)]
+    greeted += [(to_x[0] + to_z[1] + to_y[0], gy)]
+    greeted += [(x, y) for y in (partner, beside) for x in (gx, next_x, last_x)]
+    greeted += [(next_x, gy), (last_x, gy)]
+    for x, y in greeted:
+        pl.semaphore_signal(barrier, inc=1, **peer(x, y))
 
     zero_plane = jnp.zeros((cy + 2, cz, 128), BF)
     zero_row = jnp.zeros((cx + 2, 1, cz, 128), BF)
@@ -153,7 +155,7 @@
     loads[1].wait()
 
     def forward(half, save):
-        base = pl.multiple_of(half * (ny // 2) * 64, (ny // 2) * 64)
+        base = pl.multiple_of(half * nz * 64, nz * 64)
         rows = a_v[pl.ds(base, nz * 64), :]
         spins = [[eighth(((2 * (2 * z + half) + j2) * gy) % 8) for j2 in range(2)] for z in range(nz)]
         for xp in range(cx // 2):
@@ -176,14 +178,21 @@
         own1[r0 : r0 + 16, xp * 256 : xp * 256 + 256] = v
 
     forward(1 - core, save_send)
-
-    pl.semaphore_wait(barrier, nx - 1 + nz - 1 + 6)
-
-    pair = pltpu.make_async_remote_copy(
-        src_ref=snd1, dst_ref=rcv1, send_sem=pair_s, recv_sem=pair_r,
-        device_id=(gx, partner), device_id_type=MESH,
-    )
-    pair.start()
+    for load in loads[2:]:
+        load.start()
+
+    pl.semaphore_wait(barrier, len(greeted))
+
+    pairs = {}
+    for d in (2, 1, 3, 0):
+        rows = pl.ds(pl.multiple_of(((zh + d) % nz) * 64, 64), 64)
+        pairs[d] = pltpu.make_async_remote_copy(
+            src_ref=snd1.at[rows], dst_ref=rcv1.at[rows],
+            send_sem=pair_s.at[d], recv_sem=pair_r.at[d], **peer(gx, partner),
+        )
+        pairs[d].start()
+    for i in range(1, ly):
+        pl.semaphore_signal(wave.at[0], inc=1, **peer(to_x[0] + to_z[0] + to_y[i], gy))
 
     inner_x, inner_y = pl.ds(1, cx), pl.ds(1, cy)
 
@@ -203,35 +212,56 @@
             src_ref=pad.at[place(dx, cx, inner_x, True), place(dy, cy, inner_y, True)],
             dst_ref=pad.at[place(dx, cx, inner_x, False), place(dy, cy, inner_y, False)],
             send_sem=halo_s.at[n], recv_sem=halo_r.at[n],
-            device_id=((gx + dx + nx) % nx, (gy + dy + ny) % ny), device_id_type=MESH,
+            **peer((gx + dx + nx) % nx, (gy + dy + ny) % ny),
         )
         halos.append((copy, ok_send, ok_recv))
 
-        @pl.when(ok_send)
-        def _(copy=copy):
-            copy.start()
+    def start_halo(n, condition):
+        @pl.when(condition)
+        def _():
+            halos[n][0].start()
+
+    near = {6: at_y < ly - 1, 7: at_y > 0}
+    for n in (6, 7):
+        start_halo(n, halos[n][1] & near[n])
 
     forward(core, save_own)
 
-    pair.wait()
     ring = []
     for d in (2, 1, 3):
         target = (zh + d) % nz
         rows = pl.ds(pl.multiple_of(target * 64, 64), 64)
+        pairs[d].wait_recv()
         snd2[rows, :] = (own1[rows, :] + rcv1[rows, :].astype(F32)).astype(BF)
         copy = pltpu.make_async_remote_copy(
             src_ref=snd2.at[rows], dst_ref=rcv2.at[d - 1],
             send_sem=ring_s.at[d - 1], recv_sem=ring_r.at[d - 1],
-            device_id=(gx, target * 2 + core), device_id_type=MESH,
+            **peer(gx, target * 2 + core),
         )
         copy.start()
         ring.append(copy)
 
     loads[2].wait()
+    lanes = lax.broadcasted_iota(jnp.int32, (1, MY * MZ), 1)
+    mode = 2 * (2 * ((lanes // 32) % nz) + lanes // (32 * nz)) + (lanes // 16) % 2
+    spin_c, spin_s = eighth((mode * gy) % 8)
+
+    def rotate(i, carry):
+        rows = pl.ds(pl.multiple_of(i * 64, 64), 64)
+        re = b_v[rows, 0:256].astype(F32)
+        im = b_v[rows, 256:512].astype(F32)
+        brot[rows, 0:256] = (spin_c * re + spin_s * im).astype(BF)
+        brot[rows, 256:512] = (spin_c * im - spin_s * re).astype(BF)
+        return carry
+
+    lax.fori_loop(0, cells // 64, rotate, 0)
+    for load in loads[3:5]:
+        load.wait()
+
+    steps = 4
+    rows_y = cy // steps
 
     def conv_block(x, m):
-        steps = 4
-        rows_y = cy // steps
         lhs = jnp.concatenate(
             [
                 pad[x + a, pl.ds(m * rows_y + b, rows_y)].reshape(rows_y * cz, 128)
@@ -251,30 +281,22 @@
         start = pl.multiple_of(m * rows_y * cz, rows_y * cz)
         conv[x, pl.ds(start, rows_y * cz), :] = total + bias[...]
 
-    def conv_planes(first, count):
+    def conv_blocks(count, place):
         def step(i, carry):
-            conv_block(first + i // 4, i % 4)
+            conv_block(*place(i))
             return carry
 
-        lax.fori_loop(0, count * 4, step, 0)
-
-    def wait_halos(which):
-        for n in which:
-            copy, ok_send, ok_recv = halos[n]
-
-            @pl.when(ok_recv)
-            def _(copy=copy):
-                copy.wait_recv()
-
-            @pl.when(ok_send)
-            def _(copy=copy):
-                copy.wait_send()
-
-    wait_halos((0, 1))
-    conv_planes(1, 2)
-
+        lax.fori_loop(0, count, step, 0)
+
+    conv_blocks(2, lambda i: (1 + i, 1))
+
+    pl.semaphore_wait(wave.at[0], ly - 1)
+    pl.semaphore_signal(wave.at[1], inc=1, **peer(to_x[0] + to_z[1] + to_y[0], gy))
+
+    pairs[0].wait_recv()
     for copy in ring:
         copy.wait_recv()
+
     rows = pl.ds(pl.multiple_of(zh * 64, 64), 64)
     lane = lax.broadcasted_iota(jnp.int32, (32, 128), 1)
     for x in range(cx):
@@ -287,57 +309,49 @@
         stage[pl.ds(4 + x, 32, stride=8), :] = jnp.where(lane < 64, pltpu.roll(re, 64, axis=1), im)
     snda[...] = stage[...].astype(BF).reshape(nx, 4, 128)
 
+    pl.semaphore_wait(wave.at[1], 1)
+
+    hops = lambda i, n: min(i, n - i)
+    order = [(x, z, y) for x in range(lx) for z in range(lz) for y in range(ly)]
+    order.sort(key=lambda o: -(hops(o[0], lx) + hops(o[1], lz) + hops(o[2], ly)))
+
     def exchange(src, dst, number):
-        def send(i, carry):
-            to = (gx + i) % nx
+        for x, z, y in order[:-1]:
+            to = to_x[x] + to_z[z] + to_y[y]
             pltpu.make_async_remote_copy(
                 src_ref=src.at[to], dst_ref=dst.at[gx],
-                send_sem=a2a_s.at[number], recv_sem=a2a_r.at[number],
-                device_id=(to, gy), device_id_type=MESH,
+                send_sem=a2a_s.at[number], recv_sem=a2a_r.at[number], **peer(to, gy),
             ).start()
-            return carry
-
-        lax.fori_loop(1, nx, send, 0)
         dst[gx] = src[gx]
 
     def wait_exchange(src, dst, number):
         most = pl.ds(0, nx - 1)
         done = pltpu.make_async_remote_copy(
             src_ref=src.at[most], dst_ref=dst.at[most],
-            send_sem=a2a_s.at[number], recv_sem=a2a_r.at[number],
-            device_id=(gx, gy), device_id_type=MESH,
+            send_sem=a2a_s.at[number], recv_sem=a2a_r.at[number], **peer(gx, gy),
         )
         done.wait_recv()
         return done
 
     exchange(snda, rcva, 0)
 
-    wait_halos((2, 3, 4, 5, 6, 7))
-    conv_planes(0, 1)
-    conv_planes(3, 1)
-    loads[3].wait()
-    lanes = lax.broadcasted_iota(jnp.int32, (1, MY * MZ), 1)
-    mode = 2 * (2 * ((lanes // 32) % nz) + lanes // (32 * nz)) + (lanes // 16) % 2
-    spin_c, spin_s = eighth((mode * gy) % 8)
-
-    def rotate(i, carry):
-        rows = pl.ds(pl.multiple_of(i * 64, 64), 64)
-        re = b_v[rows, 0:256].astype(F32)
-        im = b_v[rows, 256:512].astype(F32)
-        brot[rows, 0:256] = (spin_c * re + spin_s * im).astype(BF)
-        brot[rows, 256:512] = (spin_c * im - spin_s * re).astype(BF)
-        return carry
-
-    lax.fori_loop(0, cells // 64, rotate, 0)
-    for load in loads[4:]:
+    for n in range(6):
+        start_halo(n, halos[n][1])
+    for n in (6, 7):
+        start_halo(n, halos[n][1] & jnp.logical_not(near[n]))
+
+    conv_blocks(2, lambda i: (1 + i, 2))
+    for load in loads[5:]:
         load.wait()
 
     first = wait_exchange(snda, rcva, 0)
+
     g = rcva[...].reshape(nx * 4, 128)
     p = jnp.dot(t_v[...], g, preferred_element_type=F32)
     lane = lax.broadcasted_iota(jnp.int32, (MX, 128), 1)
     sign = jnp.where(lane < 64, 1.0, -1.0).astype(F32)
     spec = p[:MX] + sign * pltpu.roll(p[MX:], 64, axis=1)
+
     row0 = spec * sign
     row1 = pltpu.roll(spec, 64, axis=1)
     sub = lax.broadcasted_iota(jnp.int32, (16, 128), 0) % 8
@@ -350,9 +364,20 @@
         rhs = w_v[blk * 8 : blk * 8 + 8].reshape(8 * 128, 128)
         mixed.append(jnp.dot(lhs, rhs, preferred_element_type=F32))
     mixed = jnp.concatenate(mixed, axis=0).astype(BF)
+
     back = jnp.dot(ix_v[...], mixed, preferred_element_type=F32)
     sndb[...] = back.astype(BF).reshape(nx, 8, 128)
+
     exchange(sndb, rcvb, 1)
+
+    for copy, ok_send, ok_recv in halos:
+        @pl.when(ok_recv)
+        def _(copy=copy):
+            copy.wait_recv()
+
+    conv_blocks(4, lambda i: (1 + i % 2, 3 * (i // 2)))
+    conv_blocks(4, lambda i: (0, i))
+
     second = wait_exchange(sndb, rcvb, 1)
 
     both = rcvb[...].astype(F32).reshape(nx // 2, 2, 8, 128)
@@ -363,12 +388,13 @@
             coef[q, slot, :, x * 128 : x * 128 + 128] = stage[
                 pl.ds(q * 4 + x, 32, stride=8), :
             ].astype(BF)
+
     gathers = []
     for d in (2, 1, 3):
         copy = pltpu.make_async_remote_copy(
             src_ref=coef.at[:, slot], dst_ref=coef.at[:, slot],
             send_sem=ag_s.at[d - 1], recv_sem=ag_r.at[d - 1],
-            device_id=(gx, ((zh + d) % nz) * 2 + core), device_id_type=MESH,
+            **peer(gx, ((zh + d) % nz) * 2 + core),
         )
         copy.start()
         gathers.append(copy)
@@ -378,16 +404,19 @@
         there = core * nz + (zh - d + nz) % nz
         copy = pltpu.make_async_remote_copy(
             src_ref=coef.at[:, there], dst_ref=coef.at[:, there],
-            send_sem=fw_s.at[d], recv_sem=fw_r.at[d],
-            device_id=(gx, partner), device_id_type=MESH,
+            send_sem=fw_s.at[d], recv_sem=fw_r.at[d], **peer(gx, partner),
         )
         copy.start()
         passes.append(copy)
 
     pass_on(0)
+
+    conv_blocks(4, lambda i: (cx - 1, i))
+
     for d, copy in ((1, gathers[1]), (3, gathers[2]), (2, gathers[0])):
         copy.wait_recv()
         pass_on(d)
+
     for copy in passes:
         copy.wait_recv()
 
@@ -409,10 +438,14 @@
 
     lax.fori_loop(0, parts, finish, 0)
 
-    for copy in ring + gathers + passes:
+    for copy in list(pairs.values()) + ring + gathers + passes:
         copy.wait_send()
     first.wait_send()
     second.wait_send()
+    for copy, ok_send, ok_recv in halos:
+        @pl.when(ok_send)
+        def _(copy=copy):
+            copy.wait_send()
 
 
 def body(consts, nx, ny, flow_field, spectral_weight, conv_weight, channel_bias):
@@ -425,13 +458,14 @@
     vmem = pl.BlockSpec(memory_space=pltpu.VMEM)
     out = pl.pallas_call(
         functools.partial(kernel, nx, ny),
-        out_shape=jax.ShapeDtypeStruct((cells_x, cells, channels), BF),
-        in_specs=[ANY, ANY, ANY, vmem, ANY, ANY, ANY, ANY],
+        out_shape=pltpu.VMEM((cells_x, cells, channels), BF),
+        in_specs=[ANY] * 8,
         out_specs=vmem,
         scratch_shapes=[
             v((cells_x + 2, cells_y + 2, cells_z, channels), BF),
             v((MX, 128, 128), BF),
             v((27, 128, 128), BF),
+            v((1, channels), F32),
             v((modes, cells), BF),
             v((cells, modes), BF),
             v((2 * MX, nx * cells_x), BF),
@@ -449,11 +483,12 @@
             v((nx, 8, 128), BF),
             v((2, ny, 32, cells_x * 128), BF),
             v((cells_x, cells, 128), F32),
-            dma((7,)),
+            dma((8,)),
+            pltpu.SemaphoreType.REGULAR((2,)),
             dma((8,)),
             dma((8,)),
-            dma,
-            dma,
+            dma((nz,)),
+            dma((nz,)),
             dma((nz - 1,)),
             dma((nz - 1,)),
             dma((2,)),

time: 62.4 us -> 51.8 us (0.83)
  Pallas kernels: 60 us -> 50.2 us
  local copies, waits for them, and re-layouts: 2.26 us -> 0.97 us
    pallas_call x1, Pallas kernels: 60 us -> 50.2 us  [body(): pl.pallas_call(functools.partial(kernel, nx, ny), out_shape=pltpu.VMEM((c...]
    unnamed x1, local copies, waits for them, and re-layouts: 2.26 us -> 0.97 us
where the time goes in v2:
time: 51.8 us; the launch traced here: 51.2 us
  Pallas kernels  50.2 us (97%)
  local copies, waits for them, and re-layouts  0.97 us (2%)
    pallas_call x1, Pallas kernels, body(): pl.pallas_call(functools.partial(kernel, nx, ny), out_shape=pltpu.VMEM((c...  50.2 us

profile of v2, /device:TPU:1, one launch (start us, length us, event | category | flops | bytes accessed | tf_op | source)
XLA Modules:
  0.0 51.2 jit_solution(7025128250477795062)
XLA Ops:
  0.0 50.2 %layer.1 = bf16[4,1024,128]{2,1,0:T(8,128)(2,1)S(1)} custom-call(bf16[4,16,64,128]{3,2,1,0:T(8,128)(2,1)} %flow.1, bf16[64,128,128]{2,1,0:T(8,128)(2,1)} %bitcast.5, bf16[27,128,128]{2,1,0:T(8,128)(2,1)} %bitcast.6, f32[1,128]{1,0:T(1,128)} %bitcast.7, bf16[512,1024]{1,0:T(8,128)(2,1)} %constant.8.clone.a_hbm, bf16[1024,512]{1,0:T(8,128)(2,1)} %constant.9.clone.b_hbm, ...), custom_call_target="tpu_custom_call" | custom-call | tf_op jit(solution)/shard_map/layer/pallas_call | solution.py:459
  50.3 1.0 %copy.10 = bf16[4,16,64,128]{3,2,1,0:T(8,128)(2,1)} copy(bf16[4,16,64,128]{3,2,1,0:T(8,128)(2,1)S(1)} %bitcast.4) | data formatting | bytes 2097152

commit v3 on v2

--- a/solution.py
+++ b/solution.py
@@ -61,7 +61,8 @@
     ix = np.stack([np.stack([cos, -sin]), np.stack([sin, cos])]) * MX**-0.5
     ix = ix.reshape(2, 2, count_x, cells_x, MX // 8, 8).transpose(2, 0, 3, 4, 1, 5)
     ix = ix.reshape(2 * full_x, 2 * MX)
-    return tuple(rounded(v) for v in (a, b, t, ix))
+    x = np.concatenate([ix, t[:, :128], t[:, 128:]])
+    return tuple(rounded(v) for v in (a, b, x))
 
 
 def eighth(t):
@@ -83,11 +84,11 @@
 
 def kernel(
     nx, ny,
-    flow, weight, conv_w, bias_hbm, a_hbm, b_hbm, t_hbm, ix_hbm,
+    flow, weight, conv_w, bias_hbm, a_hbm, b_hbm, x_hbm,
     out,
-    pad, w_v, cw_v, bias, a_v, b_v, t_v, ix_v, brot,
-    snd1, own1, rcv1, snd2, rcv2, stage, snda, rcva, sndb, rcvb, coef, conv,
-    load_sem, wave, halo_s, halo_r, pair_s, pair_r, ring_s, ring_r, a2a_s, a2a_r, ag_s, ag_r, fw_s, fw_r,
+    pad, w_v, cw_v, bias, a_v, b_v, x_v, brot,
+    snd1, own1, rcv1, snd2, rcv2, stage, snda, rcva, sndb, rcvb, coef, conv, sizes,
+    load_sem, wave, sent, halo_s, halo_r, pair_r, ring_r, a2a_r, ag_r, fw_r,
 ):
     gx, gy = lax.axis_index("gx"), lax.axis_index("gy")
     zh, core = gy // 2, gy % 2
@@ -102,18 +103,24 @@
     to_z = [((at_z + i) % lz) * 8 for i in range(lz)]
     to_y = [(at_y + i) % ly for i in range(ly)]
 
-    loads = [
-        pltpu.make_async_copy(flow, pad.at[pl.ds(1, cx), pl.ds(1, cy)], load_sem.at[0]),
-        pltpu.make_async_copy(a_hbm, a_v, load_sem.at[1]),
-        pltpu.make_async_copy(b_hbm, b_v, load_sem.at[2]),
-        pltpu.make_async_copy(conv_w, cw_v, load_sem.at[3]),
-        pltpu.make_async_copy(bias_hbm, bias, load_sem.at[4]),
-        pltpu.make_async_copy(t_hbm, t_v, load_sem.at[5]),
-        pltpu.make_async_copy(weight, w_v, load_sem.at[6]),
-        pltpu.make_async_copy(ix_hbm, ix_v, load_sem.at[7]),
-    ]
-    loads[0].start()
-    loads[1].start()
+    half_rows = nz * 64
+    first_rows = pl.ds(pl.multiple_of((1 - core) * half_rows, half_rows), half_rows)
+    other_rows = pl.ds(pl.multiple_of(core * half_rows, half_rows), half_rows)
+
+    def load(source, target, number):
+        return pltpu.make_async_copy(source, target, load_sem.at[number])
+
+    load_flow = load(flow, pad.at[pl.ds(1, cx), pl.ds(1, cy)], 0)
+    load_first = load(a_hbm.at[first_rows], a_v.at[first_rows], 1)
+    load_other = load(a_hbm.at[other_rows], a_v.at[other_rows], 2)
+    load_back = load(b_hbm, b_v, 0)
+    load_conv = load(conv_w, cw_v, 1)
+    load_bias = load(bias_hbm, bias, 3)
+    load_weight = load(weight, w_v, 4)
+    load_x = load(x_hbm, x_v, 5)
+    load_first.start()
+    load_flow.start()
+    load_other.start()
 
     barrier = pltpu.get_barrier_semaphore()
     partner = gy + 1 - 2 * core
@@ -151,22 +158,33 @@
     def _():
         pad[:, cy + 1 : cy + 2] = zero_row
 
-    loads[0].wait()
-    loads[1].wait()
+    load_first.wait()
+    load_flow.wait()
+
+    order_z = (2, 1, 3, 0)
+
+    def send(source, target, recv_sem, device):
+        copy = pltpu.make_async_remote_copy(
+            src_ref=source, dst_ref=target, send_sem=sent, recv_sem=recv_sem, **device
+        )
+        copy.start()
+        return copy
 
     def forward(half, save):
-        base = pl.multiple_of(half * nz * 64, nz * 64)
-        rows = a_v[pl.ds(base, nz * 64), :]
-        spins = [[eighth(((2 * (2 * z + half) + j2) * gy) % 8) for j2 in range(2)] for z in range(nz)]
+        targets = [(zh + d) % nz for d in order_z]
+        rows = jnp.concatenate(
+            [a_v[pl.ds(pl.multiple_of((half * nz + z) * 64, 64), 64), :] for z in targets], axis=0
+        )
+        spins = [[eighth(((2 * (2 * z + half) + j2) * gy) % 8) for j2 in range(2)] for z in targets]
         for xp in range(cx // 2):
             rhs = jnp.concatenate(
                 [pad[1 + 2 * xp + i, 1 : cy + 1].reshape(cells, 128) for i in range(2)], axis=1
             )
             y = jnp.dot(rows, rhs, preferred_element_type=F32)
-            for z in range(nz):
+            for n in range(nz):
                 for j2 in range(2):
-                    c, s = spins[z][j2]
-                    r0 = z * 64 + j2 * 16
+                    c, s = spins[n][j2]
+                    r0 = n * 64 + j2 * 16
                     re, im = y[r0 : r0 + 16], y[r0 + 32 : r0 + 48]
                     save(r0, xp, c * re + s * im)
                     save(r0 + 32, xp, c * im - s * re)
@@ -178,19 +196,16 @@
         own1[r0 : r0 + 16, xp * 256 : xp * 256 + 256] = v
 
     forward(1 - core, save_send)
-    for load in loads[2:]:
-        load.start()
+    for item in (load_back, load_conv, load_bias, load_weight, load_x):
+        item.start()
 
     pl.semaphore_wait(barrier, len(greeted))
 
-    pairs = {}
-    for d in (2, 1, 3, 0):
-        rows = pl.ds(pl.multiple_of(((zh + d) % nz) * 64, 64), 64)
-        pairs[d] = pltpu.make_async_remote_copy(
-            src_ref=snd1.at[rows], dst_ref=rcv1.at[rows],
-            send_sem=pair_s.at[d], recv_sem=pair_r.at[d], **peer(gx, partner),
-        )
-        pairs[d].start()
+    pair_rows = (pl.ds(0, 64), pl.ds(64, (nz - 1) * 64))
+    pairs = [
+        send(snd1.at[rows], rcv1.at[rows], pair_r.at[n], peer(gx, partner))
+        for n, rows in enumerate(pair_rows)
+    ]
     for i in range(1, ly):
         pl.semaphore_signal(wave.at[0], inc=1, **peer(to_x[0] + to_z[0] + to_y[i], gy))
 
@@ -202,46 +217,47 @@
         edge = (count if step > 0 else 1) if send else (0 if step > 0 else count + 1)
         return pl.ds(edge, 1)
 
-    halos = []
-    for n, (dx, dy) in enumerate(
-        ((0, 1), (0, -1), (1, 1), (1, -1), (-1, 1), (-1, -1), (1, 0), (-1, 0))
-    ):
-        ok_send = (gx + dx >= 0) & (gx + dx < nx) & (gy + dy >= 0) & (gy + dy < ny)
-        ok_recv = (gx - dx >= 0) & (gx - dx < nx) & (gy - dy >= 0) & (gy - dy < ny)
-        copy = pltpu.make_async_remote_copy(
+    steps = ((0, 1), (0, -1), (1, 1), (1, -1), (-1, 1), (-1, -1), (1, 0), (-1, 0))
+
+    def halo(n):
+        dx, dy = steps[n]
+        return pltpu.make_async_remote_copy(
             src_ref=pad.at[place(dx, cx, inner_x, True), place(dy, cy, inner_y, True)],
             dst_ref=pad.at[place(dx, cx, inner_x, False), place(dy, cy, inner_y, False)],
             send_sem=halo_s.at[n], recv_sem=halo_r.at[n],
             **peer((gx + dx + nx) % nx, (gy + dy + ny) % ny),
         )
-        halos.append((copy, ok_send, ok_recv))
-
-    def start_halo(n, condition):
-        @pl.when(condition)
+
+    def inside_grid(n, sign):
+        dx, dy = steps[n]
+        x, y = gx + sign * dx, gy + sign * dy
+        return (x >= 0) & (x < nx) & (y >= 0) & (y < ny)
+
+    def start_halo(n, condition=True):
+        @pl.when(inside_grid(n, 1) & condition)
         def _():
-            halos[n][0].start()
+            halo(n).start()
+
+    def wait_halo(n, condition=True):
+        @pl.when(inside_grid(n, -1) & condition)
+        def _():
+            halo(n).wait_recv()
 
     near = {6: at_y < ly - 1, 7: at_y > 0}
     for n in (6, 7):
-        start_halo(n, halos[n][1] & near[n])
-
+        start_halo(n, near[n])
+
+    load_other.wait()
     forward(core, save_own)
 
-    ring = []
-    for d in (2, 1, 3):
-        target = (zh + d) % nz
-        rows = pl.ds(pl.multiple_of(target * 64, 64), 64)
-        pairs[d].wait_recv()
+    for n, d in enumerate(order_z[:-1]):
+        rows = slice(n * 64, n * 64 + 64)
+        if n < 2:
+            pairs[n].wait_recv()
         snd2[rows, :] = (own1[rows, :] + rcv1[rows, :].astype(F32)).astype(BF)
-        copy = pltpu.make_async_remote_copy(
-            src_ref=snd2.at[rows], dst_ref=rcv2.at[d - 1],
-            send_sem=ring_s.at[d - 1], recv_sem=ring_r.at[d - 1],
-            **peer(gx, target * 2 + core),
-        )
-        copy.start()
-        ring.append(copy)
-
-    loads[2].wait()
+        send(snd2.at[rows], rcv2.at[n], ring_r, peer(gx, ((zh + d) % nz) * 2 + core))
+
+    load_back.wait()
     lanes = lax.broadcasted_iota(jnp.int32, (1, MY * MZ), 1)
     mode = 2 * (2 * ((lanes // 32) % nz) + lanes // (32 * nz)) + (lanes // 16) % 2
     spin_c, spin_s = eighth((mode * gy) % 8)
@@ -255,11 +271,10 @@
         return carry
 
     lax.fori_loop(0, cells // 64, rotate, 0)
-    for load in loads[3:5]:
-        load.wait()
-
-    steps = 4
-    rows_y = cy // steps
+    load_conv.wait()
+    load_bias.wait()
+
+    rows_y = cy // 4
 
     def conv_block(x, m):
         lhs = jnp.concatenate(
@@ -288,16 +303,19 @@
 
         lax.fori_loop(0, count, step, 0)
 
-    conv_blocks(2, lambda i: (1 + i, 1))
+    conv_blocks(4, lambda i: (1 + i // 2, 1 + i % 2))
 
     pl.semaphore_wait(wave.at[0], ly - 1)
     pl.semaphore_signal(wave.at[1], inc=1, **peer(to_x[0] + to_z[1] + to_y[0], gy))
 
-    pairs[0].wait_recv()
-    for copy in ring:
-        copy.wait_recv()
-
-    rows = pl.ds(pl.multiple_of(zh * 64, 64), 64)
+    def arrived(ref, recv_sem):
+        pltpu.make_async_remote_copy(
+            src_ref=ref, dst_ref=ref, send_sem=sent, recv_sem=recv_sem, **peer(gx, gy)
+        ).wait_recv()
+
+    arrived(rcv2, ring_r)
+
+    rows = slice((nz - 1) * 64, nz * 64)
     lane = lax.broadcasted_iota(jnp.int32, (32, 128), 1)
     for x in range(cx):
         cols = slice(x * 128, x * 128 + 128)
@@ -318,36 +336,31 @@
     def exchange(src, dst, number):
         for x, z, y in order[:-1]:
             to = to_x[x] + to_z[z] + to_y[y]
-            pltpu.make_async_remote_copy(
-                src_ref=src.at[to], dst_ref=dst.at[gx],
-                send_sem=a2a_s.at[number], recv_sem=a2a_r.at[number], **peer(to, gy),
-            ).start()
-        dst[gx] = src[gx]
-
-    def wait_exchange(src, dst, number):
-        most = pl.ds(0, nx - 1)
-        done = pltpu.make_async_remote_copy(
-            src_ref=src.at[most], dst_ref=dst.at[most],
-            send_sem=a2a_s.at[number], recv_sem=a2a_r.at[number], **peer(gx, gy),
-        )
-        done.wait_recv()
-        return done
+            send(src.at[to], dst.at[gx], a2a_r.at[number], peer(to, gy))
+
+    def wait_exchange(dst, number):
+        arrived(dst.at[pl.ds(0, nx - 1)], a2a_r.at[number])
 
     exchange(snda, rcva, 0)
-
-    for n in range(6):
-        start_halo(n, halos[n][1])
+    rcva[gx] = snda[gx]
+
     for n in (6, 7):
-        start_halo(n, halos[n][1] & jnp.logical_not(near[n]))
-
-    conv_blocks(2, lambda i: (1 + i, 2))
-    for load in loads[5:]:
-        load.wait()
-
-    first = wait_exchange(snda, rcva, 0)
+        start_halo(n, jnp.logical_not(near[n]))
+
+    low_near, high_near = near[7], near[6]
+    wait_halo(6, low_near)
+    wait_halo(7, high_near)
+    conv_blocks(jnp.where(low_near, 2, 0), lambda i: (0, 1 + i))
+    conv_blocks(jnp.where(high_near, 2, 0), lambda i: (cx - 1, 1 + i))
+    load_weight.wait()
+    load_x.wait()
+
+    wait_exchange(rcva, 0)
 
     g = rcva[...].reshape(nx * 4, 128)
-    p = jnp.dot(t_v[...], g, preferred_element_type=F32)
+    full = nx * cx
+    table = jnp.concatenate([x_v[2 * full : 2 * full + 128], x_v[2 * full + 128 :]], axis=1)
+    p = jnp.dot(table, g, preferred_element_type=F32)
     lane = lax.broadcasted_iota(jnp.int32, (MX, 128), 1)
     sign = jnp.where(lane < 64, 1.0, -1.0).astype(F32)
     spec = p[:MX] + sign * pltpu.roll(p[MX:], 64, axis=1)
@@ -365,20 +378,22 @@
         mixed.append(jnp.dot(lhs, rhs, preferred_element_type=F32))
     mixed = jnp.concatenate(mixed, axis=0).astype(BF)
 
-    back = jnp.dot(ix_v[...], mixed, preferred_element_type=F32)
+    back = jnp.dot(x_v[: 2 * full, :], mixed, preferred_element_type=F32)
     sndb[...] = back.astype(BF).reshape(nx, 8, 128)
 
     exchange(sndb, rcvb, 1)
-
-    for copy, ok_send, ok_recv in halos:
-        @pl.when(ok_recv)
-        def _(copy=copy):
-            copy.wait_recv()
-
-    conv_blocks(4, lambda i: (1 + i % 2, 3 * (i // 2)))
-    conv_blocks(4, lambda i: (0, i))
-
-    second = wait_exchange(sndb, rcvb, 1)
+    rcvb[gx] = sndb[gx]
+
+    for n in range(6):
+        start_halo(n)
+
+    wait_halo(6, jnp.logical_not(low_near))
+    wait_halo(7, jnp.logical_not(high_near))
+
+    conv_blocks(jnp.where(low_near, 0, 2), lambda i: (0, 1 + i))
+    conv_blocks(jnp.where(high_near, 0, 2), lambda i: (cx - 1, 1 + i))
+
+    wait_exchange(rcvb, 1)
 
     both = rcvb[...].astype(F32).reshape(nx // 2, 2, 8, 128)
     stage[...] = (both[:, 0] + both[:, 1]).reshape(nx // 2 * 8, 128)
@@ -389,36 +404,30 @@
                 pl.ds(q * 4 + x, 32, stride=8), :
             ].astype(BF)
 
-    gathers = []
-    for d in (2, 1, 3):
-        copy = pltpu.make_async_remote_copy(
-            src_ref=coef.at[:, slot], dst_ref=coef.at[:, slot],
-            send_sem=ag_s.at[d - 1], recv_sem=ag_r.at[d - 1],
-            **peer(gx, ((zh + d) % nz) * 2 + core),
-        )
-        copy.start()
-        gathers.append(copy)
-    passes = []
+    gathers = [
+        send(
+            coef.at[:, slot], coef.at[:, slot], ag_r.at[d - 1],
+            peer(gx, ((zh + d) % nz) * 2 + core),
+        )
+        for d in order_z[:-1]
+    ]
 
     def pass_on(d):
-        there = core * nz + (zh - d + nz) % nz
-        copy = pltpu.make_async_remote_copy(
-            src_ref=coef.at[:, there], dst_ref=coef.at[:, there],
-            send_sem=fw_s.at[d], recv_sem=fw_r.at[d], **peer(gx, partner),
-        )
-        copy.start()
-        passes.append(copy)
+        there = coef.at[:, core * nz + (zh - d + nz) % nz]
+        send(there, there, fw_r, peer(gx, partner))
 
     pass_on(0)
 
-    conv_blocks(4, lambda i: (cx - 1, i))
-
-    for d, copy in ((1, gathers[1]), (3, gathers[2]), (2, gathers[0])):
-        copy.wait_recv()
-        pass_on(d)
-
-    for copy in passes:
-        copy.wait_recv()
+    for n in range(6):
+        wait_halo(n)
+
+    conv_blocks(8, lambda i: (i % cx, 3 * (i // cx)))
+
+    for n in (1, 2, 0):
+        gathers[n].wait_recv()
+        pass_on(order_z[n])
+
+    arrived(coef.at[:, pl.ds((1 - core) * nz, nz)], fw_r)
 
     root = math.sqrt(2.0 / math.pi)
     parts = 4
@@ -432,20 +441,20 @@
             acc = jnp.dot(lhs, rhs, preferred_element_type=F32)
             for x in range(2):
                 v = acc[:, x * 128 : x * 128 + 128] + conv[2 * xp + x, rows, :]
-                v = 0.5 * v * (1.0 + jnp.tanh(root * (v + 0.044715 * (v * v * v))))
-                out[2 * xp + x, rows, :] = v.astype(BF)
+                t = jnp.tanh(v * (root + (root * 0.044715) * (v * v)))
+                v = 0.5 * v
+                out[2 * xp + x, rows, :] = (v + v * t).astype(BF)
         return carry
 
-    lax.fori_loop(0, parts, finish, 0)
-
-    for copy in list(pairs.values()) + ring + gathers + passes:
-        copy.wait_send()
-    first.wait_send()
-    second.wait_send()
-    for copy, ok_send, ok_recv in halos:
-        @pl.when(ok_send)
-        def _(copy=copy):
-            copy.wait_send()
+    lax.fori_loop(0, parts, finish, 0, unroll=True)
+
+    pltpu.make_async_remote_copy(
+        src_ref=sizes, dst_ref=sizes, send_sem=sent, recv_sem=fw_r, **peer(gx, gy)
+    ).wait_send()
+    for n in range(8):
+        @pl.when(inside_grid(n, 1))
+        def _(n=n):
+            halo(n).wait_send()
 
 
 def body(consts, nx, ny, flow_field, spectral_weight, conv_weight, channel_bias):
@@ -456,10 +465,12 @@
     v = pltpu.VMEM
     dma = pltpu.SemaphoreType.DMA
     vmem = pl.BlockSpec(memory_space=pltpu.VMEM)
+    band = 64 * cells_x // 4
+    sent_kib = band * (nz + 2 * (nz - 1) + nz) + 3 * (nx - 1)
     out = pl.pallas_call(
         functools.partial(kernel, nx, ny),
         out_shape=pltpu.VMEM((cells_x, cells, channels), BF),
-        in_specs=[ANY] * 8,
+        in_specs=[ANY] * 7,
         out_specs=vmem,
         scratch_shapes=[
             v((cells_x + 2, cells_y + 2, cells_z, channels), BF),
@@ -468,8 +479,7 @@
             v((1, channels), F32),
             v((modes, cells), BF),
             v((cells, modes), BF),
-            v((2 * MX, nx * cells_x), BF),
-            v((2 * nx * cells_x, 2 * MX), BF),
+            v((2 * nx * cells_x + 4 * MX, 2 * MX), BF),
             v((cells, modes), BF),
             v((modes // 2, cells_x * 128), BF),
             v((modes // 2, cells_x * 128), F32),
@@ -483,20 +493,17 @@
             v((nx, 8, 128), BF),
             v((2, ny, 32, cells_x * 128), BF),
             v((cells_x, cells, 128), F32),
-            dma((8,)),
+            v((sent_kib, 4, 128), BF),
+            dma((6,)),
             pltpu.SemaphoreType.REGULAR((2,)),
+            dma,
             dma((8,)),
             dma((8,)),
-            dma((nz,)),
-            dma((nz,)),
-            dma((nz - 1,)),
-            dma((nz - 1,)),
             dma((2,)),
+            dma,
             dma((2,)),
             dma((nz - 1,)),
-            dma((nz - 1,)),
-            dma((nz,)),
-            dma((nz,)),
+            dma,
         ],
         compiler_params=pltpu.CompilerParams(collective_id=0, has_side_effects=True),
         name="layer",

time: 51.8 us -> 50.1 us (0.967)
  Pallas kernels: 50.2 us -> 49 us
    pallas_call x1, Pallas kernels: 50.2 us -> 49 us  [body(): pl.pallas_call(functools.partial(kernel, nx, ny), out_shape=pltpu.VMEM((c...]
where the time goes in v3:
time: 50.1 us; the launch traced here: 50 us
  Pallas kernels  49 us (98%)
  local copies, waits for them, and re-layouts  0.97 us (2%)
    pallas_call x1, Pallas kernels, body(): pl.pallas_call(functools.partial(kernel, nx, ny), out_shape=pltpu.VMEM((c...  49 us

profile of v3, /device:TPU:1, one launch (start us, length us, event | category | flops | bytes accessed | tf_op | source)
XLA Modules:
  0.0 50.0 jit_solution(13168046097705318098)
XLA Ops:
  0.0 49.0 %layer.1 = bf16[4,1024,128]{2,1,0:T(8,128)(2,1)S(1)} custom-call(bf16[4,16,64,128]{3,2,1,0:T(8,128)(2,1)} %flow.1, bf16[64,128,128]{2,1,0:T(8,128)(2,1)} %bitcast.5, bf16[27,128,128]{2,1,0:T(8,128)(2,1)} %bitcast.6, f32[1,128]{1,0:T(1,128)} %bitcast.7, bf16[512,1024]{1,0:T(8,128)(2,1)} %constant.6.clone.a_hbm, bf16[1024,512]{1,0:T(8,128)(2,1)} %constant.7.clone.b_hbm, ...), custom_call_target="tpu_custom_call" | custom-call | tf_op jit(solution)/shard_map/layer/pallas_call | solution.py:470
  49.0 1.0 %copy.9 = bf16[4,16,64,128]{3,2,1,0:T(8,128)(2,1)} copy(bf16[4,16,64,128]{3,2,1,0:T(8,128)(2,1)S(1)} %bitcast.4) | data formatting | bytes 2097152

commit v4 on v3

--- a/solution.py
+++ b/solution.py
@@ -54,7 +54,7 @@
     a = np.stack([a_re.reshape(split), a_im.reshape(split)])
     a = a.transpose(2, 1, 0, 3, 4, 5).reshape(2 * MY * MZ, cells)
     b = np.stack([b_re.reshape(split), b_im.reshape(split)])
-    b = b.transpose(0, 2, 1, 3, 4, 5).reshape(2 * MY * MZ, cells).T
+    b = 0.5 * b.transpose(0, 2, 1, 3, 4, 5).reshape(2 * MY * MZ, cells).T
     theta = angles(signed(MX), np.arange(full_x), full_x)
     t = np.concatenate([np.cos(theta), np.sin(theta)]) * full_x**-0.5
     cos, sin = np.cos(theta.T), np.sin(theta.T)
@@ -88,7 +88,7 @@
     out,
     pad, w_v, cw_v, bias, a_v, b_v, x_v, brot,
     snd1, own1, rcv1, snd2, rcv2, stage, snda, rcva, sndb, rcvb, coef, conv, sizes,
-    load_sem, wave, sent, halo_s, halo_r, pair_r, ring_r, a2a_r, ag_r, fw_r,
+    load_sem, wave, sent, halo_s, halo_r, pair_r, ring_r, a2a_r, ag_r, own_r, fw_r,
 ):
     gx, gy = lax.axis_index("gx"), lax.axis_index("gy")
     zh, core = gy // 2, gy % 2
@@ -119,8 +119,8 @@
     load_weight = load(weight, w_v, 4)
     load_x = load(x_hbm, x_v, 5)
     load_first.start()
-    load_flow.start()
-    load_other.start()
+    for x in range(cx):
+        load(flow.at[x], pad.at[1 + x, pl.ds(1, cy)], 0).start()
 
     barrier = pltpu.get_barrier_semaphore()
     partner = gy + 1 - 2 * core
@@ -160,6 +160,7 @@
 
     load_first.wait()
     load_flow.wait()
+    load_other.start()
 
     order_z = (2, 1, 3, 0)
 
@@ -294,7 +295,7 @@
         high = pltpu.roll(acc[:, 256:384], rows_y * cz - 1, axis=0)
         total = acc[:, 128:256] + jnp.where(z == 0, 0.0, low) + jnp.where(z == cz - 1, 0.0, high)
         start = pl.multiple_of(m * rows_y * cz, rows_y * cz)
-        conv[x, pl.ds(start, rows_y * cz), :] = total + bias[...]
+        conv[x, pl.ds(start, rows_y * cz), :] = 0.5 * (total + bias[...])
 
     def conv_blocks(count, place):
         def step(i, carry):
@@ -404,30 +405,62 @@
                 pl.ds(q * 4 + x, 32, stride=8), :
             ].astype(BF)
 
-    gathers = [
-        send(
-            coef.at[:, slot], coef.at[:, slot], ag_r.at[d - 1],
-            peer(gx, ((zh + d) % nz) * 2 + core),
-        )
-        for d in order_z[:-1]
-    ]
-
-    def pass_on(d):
-        there = coef.at[:, core * nz + (zh - d + nz) % nz]
-        send(there, there, fw_r, peer(gx, partner))
-
-    pass_on(0)
+    chunk = 16 * cx
+
+    def band(owner, d):
+        return coef.at[:, owner * nz + (zh - d + nz) % nz]
+
+    def along_z(piece, number, d):
+        send(piece, piece, ag_r.at[number], peer(gx, ((zh + d) % nz) * 2 + core))
+
+    def pass_on(piece, recv_sem):
+        send(piece, piece, recv_sem, peer(gx, partner))
+
+    @pl.when(core == 0)
+    def _():
+        pass_on(band(0, 0), own_r)
+        for d in (1, 3):
+            along_z(band(0, 0), d - 1, d)
+
+    @pl.when(core == 1)
+    def _():
+        for d in (2, 1, 3):
+            along_z(band(1, 0), d - 1, d)
+        pass_on(band(1, 0), fw_r)
 
     for n in range(6):
         wait_halo(n)
 
-    conv_blocks(8, lambda i: (i % cx, 3 * (i // cx)))
-
-    for n in (1, 2, 0):
-        gathers[n].wait_recv()
-        pass_on(order_z[n])
-
-    arrived(coef.at[:, pl.ds((1 - core) * nz, nz)], fw_r)
+    conv_blocks(3, lambda i: (i, 0))
+
+    @pl.when(core == 1)
+    def _():
+        arrived(band(0, 0), own_r)
+        along_z(band(0, 0), 3, 2)
+
+    conv_blocks(5, lambda i: ((i + 3) % cx, 3 * ((i + 3) // cx)))
+
+    @pl.when(core == 0)
+    def _():
+        for d in (1, 3):
+            arrived(band(0, d), ag_r.at[d - 1])
+            pass_on(band(0, d), fw_r)
+
+    @pl.when(core == 1)
+    def _():
+        for d in (1, 3, 2):
+            arrived(band(1, d), ag_r.at[d - 1])
+            pass_on(band(1, d), fw_r)
+        arrived(band(0, 2), ag_r.at[3])
+        pass_on(band(0, 2), fw_r)
+
+    @pl.when(core == 0)
+    def _():
+        arrived(sizes.at[pl.ds(0, 5 * chunk)], fw_r)
+
+    @pl.when(core == 1)
+    def _():
+        arrived(sizes.at[pl.ds(0, 2 * chunk)], fw_r)
 
     root = math.sqrt(2.0 / math.pi)
     parts = 4
@@ -441,16 +474,20 @@
             acc = jnp.dot(lhs, rhs, preferred_element_type=F32)
             for x in range(2):
                 v = acc[:, x * 128 : x * 128 + 128] + conv[2 * xp + x, rows, :]
-                t = jnp.tanh(v * (root + (root * 0.044715) * (v * v)))
-                v = 0.5 * v
+                t = jnp.tanh(v * (2.0 * root + (8.0 * 0.044715 * root) * (v * v)))
                 out[2 * xp + x, rows, :] = (v + v * t).astype(BF)
         return carry
 
     lax.fori_loop(0, parts, finish, 0, unroll=True)
 
-    pltpu.make_async_remote_copy(
-        src_ref=sizes, dst_ref=sizes, send_sem=sent, recv_sem=fw_r, **peer(gx, gy)
-    ).wait_send()
+    def all_sent(count):
+        ref = sizes.at[pl.ds(0, count)]
+        pltpu.make_async_remote_copy(
+            src_ref=ref, dst_ref=ref, send_sem=sent, recv_sem=fw_r, **peer(gx, gy)
+        ).wait_send()
+
+    pl.when(core == 0)(lambda: all_sent(sizes.shape[0] - 4 * chunk))
+    pl.when(core == 1)(lambda: all_sent(sizes.shape[0]))
     for n in range(8):
         @pl.when(inside_grid(n, 1))
         def _(n=n):
@@ -466,7 +503,7 @@
     dma = pltpu.SemaphoreType.DMA
     vmem = pl.BlockSpec(memory_space=pltpu.VMEM)
     band = 64 * cells_x // 4
-    sent_kib = band * (nz + 2 * (nz - 1) + nz) + 3 * (nx - 1)
+    sent_kib = band * (nz + (nz - 1) + 9) + 3 * (nx - 1)
     out = pl.pallas_call(
         functools.partial(kernel, nx, ny),
         out_shape=pltpu.VMEM((cells_x, cells, channels), BF),
@@ -502,7 +539,8 @@
             dma((2,)),
             dma,
             dma((2,)),
-            dma((nz - 1,)),
+            dma((nz,)),
+            dma,
             dma,
         ],
         compiler_params=pltpu.CompilerParams(collective_id=0, has_side_effects=True),

time: 50.1 us -> 49.4 us (0.986)
  Pallas kernels: 49 us -> 48.3 us
    pallas_call x1, Pallas kernels: 49 us -> 48.3 us  [body(): pl.pallas_call(functools.partial(kernel, nx, ny), out_shape=pltpu.VMEM((c...]
where the time goes in v4:
time: 49.4 us; the launch traced here: 49.3 us
  Pallas kernels  48.3 us (98%)
  local copies, waits for them, and re-layouts  0.97 us (2%)
    pallas_call x1, Pallas kernels, body(): pl.pallas_call(functools.partial(kernel, nx, ny), out_shape=pltpu.VMEM((c...  48.3 us

profile of v4, /device:TPU:1, one launch (start us, length us, event | category | flops | bytes accessed | tf_op | source)
XLA Modules:
  0.0 49.3 jit_solution(7170089334235572040)
XLA Ops:
  0.0 48.3 %layer.1 = bf16[4,1024,128]{2,1,0:T(8,128)(2,1)S(1)} custom-call(bf16[4,16,64,128]{3,2,1,0:T(8,128)(2,1)} %flow.1, bf16[64,128,128]{2,1,0:T(8,128)(2,1)} %bitcast.5, bf16[27,128,128]{2,1,0:T(8,128)(2,1)} %bitcast.6, f32[1,128]{1,0:T(1,128)} %bitcast.7, bf16[512,1024]{1,0:T(8,128)(2,1)} %constant.6.clone.a_hbm, bf16[1024,512]{1,0:T(8,128)(2,1)} %constant.7.clone.b_hbm, ...), custom_call_target="tpu_custom_call" | custom-call | tf_op jit(solution)/shard_map/layer/pallas_call | solution.py:507
  48.3 1.0 %copy.9 = bf16[4,16,64,128]{3,2,1,0:T(8,128)(2,1)} copy(bf16[4,16,64,128]{3,2,1,0:T(8,128)(2,1)S(1)} %bitcast.4) | data formatting | bytes 2097152

commit v5 on v4

--- a/solution.py
+++ b/solution.py
@@ -428,17 +428,15 @@
             along_z(band(1, 0), d - 1, d)
         pass_on(band(1, 0), fw_r)
 
+    @pl.when(core == 1)
+    def _():
+        arrived(band(0, 0), own_r)
+        along_z(band(0, 0), 3, 2)
+
     for n in range(6):
         wait_halo(n)
 
-    conv_blocks(3, lambda i: (i, 0))
-
-    @pl.when(core == 1)
-    def _():
-        arrived(band(0, 0), own_r)
-        along_z(band(0, 0), 3, 2)
-
-    conv_blocks(5, lambda i: ((i + 3) % cx, 3 * ((i + 3) // cx)))
+    conv_blocks(8, lambda i: (i % cx, 3 * (i // cx)))
 
     @pl.when(core == 0)
     def _():

time: 49.4 us -> 49.4 us (level)
  no operation moved by 1% of the time
where the time goes in v5:
time: 49.4 us; the launch traced here: 49.3 us
  Pallas kernels  48.3 us (98%)
  local copies, waits for them, and re-layouts  0.97 us (2%)
    pallas_call x1, Pallas kernels, body(): pl.pallas_call(functools.partial(kernel, nx, ny), out_shape=pltpu.VMEM((c...  48.3 us

profile of v5, /device:TPU:1, one launch (start us, length us, event | category | flops | bytes accessed | tf_op | source)
XLA Modules:
  0.0 49.3 jit_solution(15630012639985309815)
XLA Ops:
  0.0 48.3 %layer.1 = bf16[4,1024,128]{2,1,0:T(8,128)(2,1)S(1)} custom-call(bf16[4,16,64,128]{3,2,1,0:T(8,128)(2,1)} %flow.1, bf16[64,128,128]{2,1,0:T(8,128)(2,1)} %bitcast.5, bf16[27,128,128]{2,1,0:T(8,128)(2,1)} %bitcast.6, f32[1,128]{1,0:T(1,128)} %bitcast.7, bf16[512,1024]{1,0:T(8,128)(2,1)} %constant.6.clone.a_hbm, bf16[1024,512]{1,0:T(8,128)(2,1)} %constant.7.clone.b_hbm, ...), custom_call_target="tpu_custom_call" | custom-call | tf_op jit(solution)/shard_map/layer/pallas_call | solution.py:505
  48.3 1.0 %copy.9 = bf16[4,16,64,128]{3,2,1,0:T(8,128)(2,1)} copy(bf16[4,16,64,128]{3,2,1,0:T(8,128)(2,1)S(1)} %bitcast.4) | data formatting | bytes 2097152
